TPU v7x, 1024 devices: a whole 4x4x32 slice. The times are simulated.
1024 devices in a mesh: ctx: 16 (over x, y), ch: 64 (over z, core).
Axes of the slice: x: 4, y: 4, z: 32, core: 2. Of those that a mesh axis runs over, the one named last changes fastest.
Arguments:
- proj: bfloat16 [3, 4096, 4096], P(None, 'ch', 'ctx'), may hold values from -4 to 4
- scale_exp: int32 [3, 4096, 32], P(None, 'ch', 'ctx'), may hold values from -1 to 1
- filt: bfloat16 [4096, 4096], P('ch'), may hold values from -8 to 8
- reach: int32 [4096], P('ch'), may hold values from 0 to 4
- skip: float32 [4096], P('ch'), may hold values from 0.1 to 1.9
- cotangent: bfloat16 [4096, 4096], P('ch', 'ctx'), may hold values from -6 to 6
Outputs:
- scaled_out: bfloat16 [4096, 4096], P('ch', 'ctx')
- token_max: float32 [4096], P('ctx')
- gradients: bfloat16 [3, 4096, 4096], P(None, 'ch', 'ctx')
- filter_grad: float32 [4096, 4096], P('ch', 'ctx')
All inputs are finite; a program needn't handle non-finite values. Where the computation divides by a largest or mean magnitude, that divisor is 1e-20 or more.
Results may differ from a plain program's by a relative error of at most 0.015.
Values may be sent and summed in bfloat16 or wider, within the bound.
A program may use at most 32 MiB of HBM per device.

v0:
```python
import math

import jax
import jax.numpy as jnp
from jax import lax
from jax.sharding import PartitionSpec as P

REACH_DIVISORS = (64, 32, 16, 4, 1)


def fourier_basis(span_len):
    freq_index = jnp.arange(span_len, dtype=jnp.int32)
    phase = (2 * freq_index[None, :] + 1) * freq_index[:, None] % (4 * span_len)
    angle = phase.astype(jnp.float32) * (math.pi / (2 * span_len))
    return jnp.concatenate([jnp.cos(angle), -jnp.sin(angle)], axis=1)


def to_spectrum(signal, basis):
    return jnp.einsum("...s,sf->...f", signal, basis, precision=lax.Precision.HIGHEST)


def from_spectrum(spectrum, basis):
    return (
        jnp.einsum("...f,sf->...s", spectrum, basis, precision=lax.Precision.HIGHEST)
        / basis.shape[0]
    )


def blocks_spectrum(signal, basis, channels, blocks_in, span_len):
    shaped = signal.reshape(channels, blocks_in, span_len)
    return jnp.einsum("cks,sf->kcf", shaped, basis, precision=lax.Precision.HIGHEST)


def complex_mul(first_op, second_op):
    half_len = first_op.shape[-1] // 2
    real_a = first_op[..., :half_len]
    imag_a = first_op[..., half_len:]
    real_b = second_op[..., :half_len]
    imag_b = second_op[..., half_len:]
    return jnp.concatenate(
        [real_a * real_b - imag_a * imag_b, real_a * imag_b + imag_a * real_b], axis=-1
    )


def conjugate(spectrum):
    half_len = spectrum.shape[-1] // 2
    return jnp.concatenate([spectrum[..., :half_len], -spectrum[..., half_len:]], axis=-1)


def rotate(spectrum, parity):
    half_len = spectrum.shape[-1] // 2
    return jnp.concatenate(
        [spectrum[..., half_len:] * parity, -spectrum[..., :half_len] * parity], axis=-1
    )


def unrotate(spectrum, parity):
    half_len = spectrum.shape[-1] // 2
    return jnp.concatenate(
        [-spectrum[..., half_len:] * parity, spectrum[..., :half_len] * parity], axis=-1
    )


def body(proj, scale_exp, filt, reach, skip, cotangent):
    groups, channels, span_len = proj.shape
    ctx_count = lax.axis_size("ctx")
    ctx_index = lax.axis_index("ctx")
    seq_len = ctx_count * span_len
    blocks_per = scale_exp.shape[2]
    block_len = span_len // blocks_per
    scaled = jnp.exp2(scale_exp.astype(jnp.float32))
    dequant = (
        proj.astype(jnp.float32).reshape(groups, channels, blocks_per, block_len)
        * scaled[..., None]
    ).reshape(groups, channels, span_len)
    queries = dequant[0]
    keys_deq = dequant[1]
    values_deq = dequant[2]
    mixed_bf = (keys_deq * values_deq).astype(jnp.bfloat16)
    mixed_f = lax.optimization_barrier(mixed_bf).astype(jnp.float32)
    basis = fourier_basis(span_len)
    parity = 1.0 - 2.0 * (jnp.arange(span_len, dtype=jnp.int32) % 2).astype(jnp.float32)
    divisors = jnp.array(REACH_DIVISORS, dtype=jnp.int32)
    class_ids = jnp.arange(len(REACH_DIVISORS), dtype=jnp.int32)
    reach_div = jnp.sum(
        jnp.where(reach[:, None] == class_ids[None, :], divisors[None, :], 0), axis=1
    )
    reach_len = seq_len // reach_div
    fscale = 1.0 / math.sqrt(seq_len)
    tap_index = jnp.arange(seq_len, dtype=jnp.int32)
    kernel = (
        filt.astype(jnp.float32)
        * fscale
        * (tap_index[None, :] < reach_len[:, None]).astype(jnp.float32)
    )
    block_spec = blocks_spectrum(kernel, basis, channels, ctx_count, span_len)
    empty = jnp.zeros((1, channels, 2 * span_len), jnp.float32)
    window = jnp.concatenate([empty, block_spec[:-1]], axis=0) + rotate(block_spec, parity)
    zeros_all = jnp.zeros_like(window)
    ahead_win = lax.dynamic_slice_in_dim(
        jnp.concatenate([zeros_all, window], axis=0), ctx_count - ctx_index, ctx_count, 0
    )
    own_spec = to_spectrum(mixed_f, basis)
    pieces = from_spectrum(unrotate(complex_mul(own_spec[None], ahead_win), parity), basis)
    received = lax.all_to_all(pieces, "ctx", split_axis=0, concat_axis=0, tiled=True)
    conv_out = jnp.sum(received, axis=0) + skip[:, None] * mixed_f
    response = queries * conv_out
    local_peak = jnp.max(jnp.abs(response), axis=0)
    token_max = lax.pmax(local_peak, "ch")
    scaled_out = (response / (token_max + 1e-06)[None, :]).astype(jnp.bfloat16)
    upstream = cotangent.astype(jnp.float32)
    pulled_bf = (upstream * queries).astype(jnp.bfloat16)
    pulled = lax.optimization_barrier(pulled_bf).astype(jnp.float32)
    shard_piece = lax.all_gather(pulled_bf, "ctx", axis=1, tiled=True)
    blocks_in = shard_piece.shape[1] // span_len
    later_spec = blocks_spectrum(
        shard_piece.astype(jnp.float32), basis, channels, blocks_in, span_len
    )
    back_spec = jnp.sum(complex_mul(rotate(later_spec, parity), conjugate(ahead_win)), axis=0)
    grad_mixed = from_spectrum(back_spec, basis) + skip[:, None] * pulled
    gradients = jnp.stack(
        [upstream * conv_out, grad_mixed * values_deq, grad_mixed * keys_deq]
    ).astype(jnp.bfloat16)
    padded_later = jnp.concatenate([later_spec, jnp.zeros_like(later_spec)], axis=0)
    near_spec = lax.dynamic_slice_in_dim(padded_later, ctx_index, ctx_count, 0)
    next_spec = lax.dynamic_slice_in_dim(padded_later, ctx_index + 1, ctx_count, 0)
    near_plus = near_spec + rotate(next_spec, parity)
    tap_spec = complex_mul(conjugate(own_spec)[None], near_plus)
    own_taps = lax.psum_scatter(
        from_spectrum(tap_spec, basis).astype(jnp.bfloat16), "ctx", scatter_dimension=0, tiled=True
    ).astype(jnp.float32)[0]
    own_reach = (ctx_index * span_len + jnp.arange(span_len, dtype=jnp.int32))[None, :] < reach_len[
        :, None
    ]
    filter_grad = own_taps * fscale * own_reach.astype(jnp.float32)
    return (scaled_out, token_max, gradients, filter_grad)


def solution(mesh):
    return jax.shard_map(
        body,
        mesh=mesh,
        in_specs=(
            P(None, "ch", "ctx"),
            P(None, "ch", "ctx"),
            P("ch", None),
            P("ch"),
            P("ch"),
            P("ch", "ctx"),
        ),
        out_specs=(P("ch", "ctx"), P("ctx"), P(None, "ch", "ctx"), P("ch", "ctx")),
        check_vma=False,
    )
```

profile of v0, /device:TPU:1, one launch (start us, length us, event | category | flops | bytes accessed | tf_op | source)
XLA Modules:
  0.0 185.4 jit_solution(7736295129822006831)
XLA Ops:
  7.2 1.0 fusion.38
  8.2 0.8 select_reduce_fusion
  9.0 0.1 and_select_fusion.1
  9.1 1.2 multiply_select_fusion
  10.4 1.9 %convolution_bitcast_fusion = f32[16,64,512]{2,1,0:T(8,128)S(1)} fusion(f32[8,16,8,256]{3,2,1,0:T(8,128)S(1)} %bitcast.72, f32[256,256]{1,0:T(8,128)S(1)} %get-tuple-element.30, f32[256,256]{1,0:T(8,128)S(1)} %get-tuple-element.29), kind=kOutput, calls=%fused_computation.16 | convolution fusion | flops 1610743808 | bytes 3670016 | tf_op jit(solution)/shard_map/cks,sf->kcf/dot_general | solution.py:31
  12.2 1.5 slice.89
  13.8 0.0 copy-start.1
  13.8 0.0 copy-start.4
  13.8 1.5 slice_multiply_fusion.1
  15.3 0.0 copy-start
  15.3 0.0 copy-done.1
  15.3 0.1 reshape.72
  15.4 0.0 copy-done.4
  15.4 0.1 copy.19
  15.6 0.3 broadcast_multiply_fusion
  15.9 0.3 fusion.44
  16.2 0.0 copy-done
  16.3 20.2 %all_gather.3 = bf16[64,4096]{1,0:T(8,128)(2,1)S(1)} all-gather(bf16[64,256]{1,0:T(8,128)(2,1)S(1)} %fusion.40), channel_id=1, replica_groups=mesh['ctx'=16,'ch'=64] {'ctx'}, dimensions={1}, use_global_device_ids=true | all-gather | bytes 557056 | tf_op jit(solution)/shard_map/all_gather | solution.py:114
  36.5 1.0 convolution_bitcast_fusion.1
  37.6 2.6 %maximum_add_fusion = f32[16,64,512]{2,1,0:T(8,128)S(1)} fusion(f32[16,64,256]{2,1,0:T(8,128)} %get-tuple-element.15, f32[16,64,256]{2,1,0:T(8,128)} %get-tuple-element.14, f32[15,64,512]{2,1,0:T(8,128)} %slice.89), kind=kLoop, calls=%fused_computation.6 | loop fusion | flops 1048576 | bytes 6160384 | tf_op jit(solution)/shard_map/add | solution.py:98
  40.2 2.9 %multiply_subtract_fusion.1 = (f32[16,64,256]{2,1,0:T(8,128)}, f32[16,64,256]{2,1,0:T(8,128)}, f32[16,64,256]{2,1,0:T(8,128)}, f32[16,64,256]{2,1,0:T(8,128)S(1)...) fusion(f32[16,64,512]{2,1,0:T(8,128)S(1)} %convolution_bitcast_fusion.1, f32[256]{0:T(256)S(1)} %fusion.50, ...), kind=kLoop, calls=%fused_computation.37 | loop fusion | flops 6029312 | bytes 12715020 | tf_op jit(solution)/shard_map/sub | solution.py:41
  43.1 2.9 %fusion.12 = f32[16,64,256]{2,1,0:T(8,128)} fusion(f32[16,64,256]{2,1,0:T(8,128)S(1)} %get-tuple-element.11, f32[16,64,256]{2,1,0:T(8,128)S(1)} %get-tuple-element.12, f32[256,256]{1,0:T(8,128)S(1)} %get-tuple-element.30, f32[256,256]{1,0:T(8,128)S(1)} %get-tuple-element.29), kind=kOutput, calls=%fused_computation.19 | convolution fusion | flops 1611530240 | bytes 3670016 | tf_op jit(solution)/shard_map/...f,sf->...s/dot_general | solution.py:24
  45.9 4.7 %all-to-all-start = ((f32[16,64,256]{2,1,0:T(8,128)}), f32[16,64,256]{2,1,0:T(8,128)}, u32[]{:S(2)}, u32[]{:S(2)}) async-start(f32[16,64,256]{2,1,0:T(8,128)} %fusion.12), calls=%async_computation | async-start | bytes 2097152 | tf_op jit(solution)/shard_map/all_to_all | solution.py:105
  50.6 0.2 reduce-scatter.4.cloned.1.call-start
  50.9 2.8 %fusion = (f32[16,64,512]{2,1,0:T(8,128)S(1)}, f32[64,512]{1,0:T(8,128)S(1)}) fusion(s32[]{:T(128)S(6)} %select_n.60, f32[16,64,512]{2,1,0:T(8,128)S(1)} %convolution_bitcast_fusion.1, f32[16,64,256]{2,1,0:T(8,128)} %get-tuple-element.13, f32[16,64,256]{2,1,0:T(8,128)} %get-tuple-element.10, f32[16,64,256]{2,1,0:T(8,128)} %get-tuple-element.5, ...), kind=kLoop, calls=%fused_computation.5 | loop fusion | flops 2064384 | bytes 8519684 | tf_op jit(solution)/shard_map/add | solution.py:127
  53.7 0.3 multiply_subtract_fusion
  54.0 0.0 copy-start.2
  54.0 2.6 %fusion.15 = bf16[16,64,256]{2,1,0:T(8,128)(2,1)} fusion(f32[16,64,256]{2,1,0:T(8,128)S(1)} %get-tuple-element.9, f32[16,64,256]{2,1,0:T(8,128)S(1)} %get-tuple-element.8, f32[256,256]{1,0:T(8,128)S(1)} %get-tuple-element.30, f32[256,256]{1,0:T(8,128)S(1)} %get-tuple-element.29), kind=kOutput, calls=%fused_computation.20 | convolution fusion | flops 1611792384 | bytes 3145728 | tf_op jit(solution)/shard_map/...f,sf->...s/dot_general | solution.py:24
  56.6 0.0 reduce-scatter.4.cloned.1.call-update
  56.7 0.0 copy-done.2
  56.7 0.6 fusion.46
  57.3 5.1 %all-to-all-done = f32[16,64,256]{2,1,0:T(8,128)} async-done(((f32[16,64,256]{2,1,0:T(8,128)}), f32[16,64,256]{2,1,0:T(8,128)}, u32[]{:S(2)}, u32[]{:S(2)}) %all-to-all-start) | async-done | bytes 1048608 | tf_op jit(solution)/shard_map/all_to_all | solution.py:105
  62.4 1.3 reduce_sum.28
  63.7 0.1 abs_reduce_fusion
  63.8 111.9 %pmax.7 = f32[256]{0:T(256)S(1)} all-reduce(f32[256]{0:T(256)S(1)} %abs_reduce_fusion), channel_id=1, replica_groups=mesh['ctx'=16,'ch'=64] {'ch'}, use_global_device_ids=true, to_apply=%region_3.4 | all-reduce | flops 256 | bytes 2048 | tf_op jit(solution)/shard_map/pmax | solution.py:109
  175.7 0.0 copy-start.3
  175.7 0.7 fusion.47
  176.4 0.7 pad_maximum_fusion.1
  177.1 0.0 reduce-scatter.4.cloned.1.call-done
  177.1 1.5 bitcast_select_fusion
  178.5 0.0 copy-done.3
  (12 shorter events, 0.1 us)
Async XLA Ops:
  13.8 1.5 copy-start.1
  13.8 1.6 copy-start.4
  15.3 0.9 copy-start
  45.9 16.5 %all-to-all-start = ((f32[16,64,256]{2,1,0:T(8,128)}), f32[16,64,256]{2,1,0:T(8,128)}, u32[]{:S(2)}, u32[]{:S(2)}) async-start(f32[16,64,256]{2,1,0:T(8,128)} %fusion.12), calls=%async_computation | async-start | bytes 2097152 | tf_op jit(solution)/shard_map/all_to_all | solution.py:105
  50.6 126.5 %reduce-scatter.4.cloned.1.call-start = ((), (), s32[]{:S(2)}) async-start(), calls=%async_computation.2 | async-start | bytes 557056
  54.0 2.7 %copy-start.2 = (f32[64]{0:T(128)S(1)}, f32[64]{0:T(128)}, u32[]{:S(2)}) copy-start(f32[64]{0:T(128)} %param.11) | copy-start | bytes 772
  175.7 2.8 %copy-start.3 = (f32[256]{0:T(256)}, f32[256]{0:T(256)S(1)}, u32[]{:S(2)}) copy-start(f32[256]{0:T(256)S(1)} %pmax.7) | copy-start | bytes 3076
Sparse Core Ops, SparseCore 0:
  56.8 119.6 reduce-scatter.3
where the time goes:
time: 186 us; the launch traced here: 185 us
  blocking collectives  132 us (71%)
  other arithmetic  17.8 us (10%)
  between operations  14.2 us (8%)
  matrix products  9.36 us (5%)
  waiting for transfers between devices  5.14 us (3%)
  starting transfers between devices  4.93 us (3%)
    pmax x1, blocking collectives, body(): token_max = lax.pmax(local_peak, 'ch')  112 us
    all_gather x1, blocking collectives, body(): shard_piece = lax.all_gather(pulled_bf, 'ctx', axis=1, tiled=True)  20.2 us
    dot_general x3, matrix products, from_spectrum(): jnp.einsum('...f,sf->...s', spectrum, basis, precision=lax.Precision.HIGH...  6.11 us
    all_to_all x1, waiting for transfers between devices, body(): lax.all_to_all(pieces, 'ctx', split_axis=0, concat_axis=0, tiled=True)  5.13 us
    all_to_all x1, starting transfers between devices, body(): lax.all_to_all(pieces, 'ctx', split_axis=0, concat_axis=0, tiled=True)  4.7 us
  transfers between devices with their start and end apart: 2, of which 1 were waited for; matrix products, arithmetic and copies ran while one was open for 5% of the time, Pallas kernels for 0%

commit v1 on v0

v1 whole, which is shorter than its diff:
```python
import functools
import math

import jax
import jax.numpy as jnp
from jax import lax
from jax.experimental import pallas as pl
from jax.experimental.pallas import tpu as pltpu
from jax.sharding import PartitionSpec as P

REACH_DIVISORS = (64, 32, 16, 4, 1)
MESH = pl.DeviceIdType.MESH
LANES = 128
CORES = 2
NT = (((1,), (1,)), ((), ()))


def z_windows(chips):
    if chips == 32:
        return tuple(range(-5, 6)), (0, -11, 11)
    return tuple(range(chips)), (0,)


def fine_shifts(row, dst):
    width = row.shape[1]
    strip = pltpu.roll(jnp.broadcast_to(row, (8, width)), 0, 1, stride=1, stride_axis=0)
    lane = lax.broadcasted_iota(jnp.int32, (16, LANES), 1)
    sub = lax.broadcasted_iota(jnp.int32, (16, LANES), 0)
    for k in range(LANES // 16):
        low = strip if k == 0 else pltpu.roll(strip, 16 * k, 1)
        both = jnp.concatenate([low, pltpu.roll(strip, 16 * k + 8, 1)], axis=0)
        first = jnp.where(lane >= sub + 16 * k, both[:, :LANES], 0.0)
        dst[16 * k : 16 * k + 16, :LANES] = first.astype(jnp.bfloat16)
        dst[16 * k : 16 * k + 16, LANES:] = both[:, LANES:].astype(jnp.bfloat16)


def kernel(
    parts, chips, chans, seq,
    aux, proj, cot, filt,
    so_ref, tm_ref, gr_ref, fg_ref,
    send_m, send_p, send_y, send_g, send_f,
    recv_m, recv_p, recv_y, recv_g, recv_f,
    taps_bf, taps, fine, pads, left, rev,
    lm, win1, wsend, win2,
    taps_sem, ctx_send, ctx_recv, s1_send, s1_recv, s2_send, s2_recv,
):
    own = chans // parts
    rows = 2 * own
    fscale = 1.0 / math.sqrt(seq)
    me = lax.axis_index("ctx")
    ch = lax.axis_index("ch")
    zpos = ch // CORES
    core = ch % CORES
    off1, off2 = z_windows(chips)
    n1, n2 = len(off1), len(off2)
    self1 = off1.index(0)

    def peer_of(step):
        return lax.rem(me + step, parts)

    def chip_dev(offset, side):
        return {"ch": lax.rem(zpos + (offset + chips), chips) * CORES + side}

    per_tile = 16 // own
    tile = pl.multiple_of(me // per_tile * 16, 16)
    tap_copy = pltpu.make_async_copy(filt.at[pl.ds(tile, 16), :], taps_bf, taps_sem)
    tap_copy.start()

    barrier = pltpu.get_barrier_semaphore()

    def greet(step, carry):
        pl.semaphore_signal(barrier, inc=1, device_id={"ctx": peer_of(step)}, device_id_type=MESH)
        return carry

    lax.fori_loop(1, parts, greet, 0)
    greeted = parts - 1
    for offset in off1 + off2[1:]:
        if offset == 0:
            pl.semaphore_signal(barrier, inc=1, device_id=chip_dev(0, 1 - core), device_id_type=MESH)
            greeted += 1
        else:
            for side in range(CORES):
                pl.semaphore_signal(barrier, inc=1, device_id=chip_dev(offset, side), device_id_type=MESH)
                greeted += 1

    def column(index):
        return aux[:, index : index + 1]

    def dequant(group, half):
        values = proj[group, :, LANES * half : LANES * (half + 1)].astype(jnp.float32)
        return values * column(2 * group + half)

    def upstream(half):
        return cot[:, LANES * half : LANES * (half + 1)].astype(jnp.float32)

    def mixed_of(half):
        return (dequant(1, half) * dequant(2, half)).astype(jnp.bfloat16).astype(jnp.float32)

    def pulled_of(half):
        return (upstream(half) * dequant(0, half)).astype(jnp.bfloat16).astype(jnp.float32)

    for half in range(2):
        send_m[pl.ds(half, chans, stride=2), :] = mixed_of(half)
        send_p[pl.ds(half, chans, stride=2), :] = pulled_of(half)

    mine = pl.ds(pl.multiple_of(rows * me, rows), rows)

    def exchange(which, src, dst):
        def copy(step):
            peer = peer_of(step)
            return pltpu.make_async_remote_copy(
                src_ref=src.at[pl.ds(pl.multiple_of(rows * peer, rows), rows), :],
                dst_ref=dst.at[mine, :],
                send_sem=ctx_send.at[which, peer],
                recv_sem=ctx_recv.at[which, me],
                device_id={"ctx": peer},
                device_id_type=MESH,
            )

        def arrival(step):
            peer = peer_of(step)
            return pltpu.make_async_remote_copy(
                src_ref=src.at[mine, :],
                dst_ref=dst.at[pl.ds(pl.multiple_of(rows * peer, rows), rows), :],
                send_sem=ctx_send.at[which, me],
                recv_sem=ctx_recv.at[which, peer],
                device_id={"ctx": peer},
                device_id_type=MESH,
            )

        def start():
            def go(step, carry):
                copy(step).start()
                return carry

            lax.fori_loop(1, parts, go, 0)
            dst[mine, :] = src[mine, :]

        def wait_recv():
            def go(step, carry):
                arrival(step).wait_recv()
                return carry

            lax.fori_loop(1, parts, go, 0)

        def wait_send():
            def go(step, carry):
                copy(step).wait_send()
                return carry

            lax.fori_loop(1, parts, go, 0)

        return start, wait_recv, wait_send

    m_start, m_recv, m_sent = exchange(0, send_m, recv_m)
    p_start, p_recv, p_sent = exchange(1, send_p, recv_p)
    y_start, y_recv, y_sent = exchange(2, send_y, recv_y)
    g_start, g_recv, g_sent = exchange(3, send_g, recv_g)
    f_start, f_recv, f_sent = exchange(4, send_f, recv_f)

    pl.semaphore_wait(barrier, greeted)
    m_start()
    p_start()

    tap_copy.wait()
    taps[...] = taps_bf[...].astype(jnp.float32)
    lag = lax.broadcasted_iota(jnp.int32, (1, seq), 1).astype(jnp.float32)
    for j in range(own):
        row = taps[pl.ds(me % per_tile * own + j, 1), :]
        reach = aux[pl.ds(me * own + j, 1), :][:, 7:8]
        fine_shifts(jnp.where(lag < reach, row, 0.0), fine.at[j, 0:LANES])

    flip = (
        lax.broadcasted_iota(jnp.int32, (LANES, LANES), 0)
        + lax.broadcasted_iota(jnp.int32, (LANES, LANES), 1)
        == LANES - 1
    ).astype(jnp.float32).astype(jnp.bfloat16)

    def reverse(values):
        return jnp.dot(values, flip, preferred_element_type=jnp.float32)

    m_recv()
    rev[...] = reverse(recv_m[...].astype(jnp.bfloat16))
    zeros = jnp.zeros((parts, LANES), jnp.float32)
    for slot in range(2):
        pads[slot, 0:parts, :] = zeros
    for j in range(own):
        pads[0, parts : 2 * parts, :] = rev[pl.ds(2 * j + 1, parts, stride=rows), :]
        pads[1, parts : 2 * parts, :] = rev[pl.ds(2 * j, parts, stride=rows), :]
        for n in range(2 * parts + 1):
            at = parts - n // 2
            block = pads[n % 2, at : at + parts, :].astype(jnp.bfloat16)
            if n < 2 * parts:
                left[0:parts, LANES * n : LANES * (n + 1)] = block
            if n >= 1:
                left[parts : 2 * parts, LANES * (n - 1) : LANES * n] = block
        out = lax.dot_general(left[...], fine[j, 0:LANES, :], NT, preferred_element_type=jnp.float32)
        top = out.astype(jnp.bfloat16)
        rest = (out - top.astype(jnp.float32)).astype(jnp.bfloat16)
        back = reverse(top) + reverse(rest)
        send_y[pl.ds(2 * j, parts, stride=rows), :] = back[parts:]
        send_y[pl.ds(2 * j + 1, parts, stride=rows), :] = back[:parts]
    y_start()

    def gradients_of(j):
        blocks = [recv_m[rows * c + 2 * j + half : rows * c + 2 * j + half + 1, :] for c in range(parts) for half in range(2)]
        fine_shifts(jnp.concatenate(blocks, axis=1), fine.at[j, LANES : 2 * LANES])
        for half in range(2):
            pads[half, 0:parts, :] = recv_p[pl.ds(2 * j + half, parts, stride=rows), :]
            pads[half, parts : 2 * parts, :] = zeros
        for n in range(2 * parts + 1):
            at = n // 2
            block = pads[n % 2, at : at + parts, :].astype(jnp.bfloat16)
            if n < 2 * parts:
                left[0:parts, LANES * n : LANES * (n + 1)] = block
            if n >= 1:
                left[parts : 2 * parts, LANES * (n - 1) : LANES * n] = block
        out = lax.dot_general(left[...], fine[j], NT, preferred_element_type=jnp.float32)
        for half in range(2):
            part = out[parts * half : parts * (half + 1)]
            send_g[pl.ds(2 * j + half, parts, stride=rows), :] = part[:, :LANES]
            send_f[pl.ds(2 * j + half, parts, stride=rows), :] = part[:, LANES:]

    p_recv()
    for j in range(own // 2):
        gradients_of(j)

    y_recv()
    gain = column(6)

    def conv_of(half):
        return recv_y[pl.ds(half, chans, stride=2), :] * fscale + gain * mixed_of(half)

    for half in range(2):
        peak = jnp.max(jnp.abs(dequant(0, half) * conv_of(half)), axis=0, keepdims=True)
        lm[half] = peak

    def push1(index, side):
        return pltpu.make_async_remote_copy(
            src_ref=lm.at[side],
            dst_ref=win1.at[CORES * index + core],
            send_sem=s1_send.at[CORES * index + side],
            recv_sem=s1_recv.at[CORES * index + core],
            device_id=chip_dev(off1[index], side),
            device_id_type=MESH,
        )

    def land1(index, side):
        return pltpu.make_async_remote_copy(
            src_ref=lm.at[core],
            dst_ref=win1.at[CORES * index + side],
            send_sem=s1_send.at[CORES * index + core],
            recv_sem=s1_recv.at[CORES * index + side],
            device_id=chip_dev(off1[index], side),
            device_id_type=MESH,
        )

    def sides(index, home):
        return (1 - core,) if index == home else tuple(range(CORES))

    for index in range(n1):
        for side in sides(index, self1):
            push1(index, side).start()
    win1[CORES * self1 + core] = lm[core]

    for j in range(own // 2, own):
        gradients_of(j)
    g_start()
    f_start()

    for index in range(n1):
        for side in sides(index, self1):
            land1(index, side).wait_recv()
    wide = jnp.max(win1[...], axis=0)
    wsend[0] = wide

    def push2(index, side):
        return pltpu.make_async_remote_copy(
            src_ref=wsend.at[0],
            dst_ref=win2.at[n2 * core + index],
            send_sem=s2_send.at[CORES * index + side],
            recv_sem=s2_recv.at[n2 * core + index],
            device_id=chip_dev(off2[index], side),
            device_id_type=MESH,
        )

    def land2(index, side):
        return pltpu.make_async_remote_copy(
            src_ref=wsend.at[0],
            dst_ref=win2.at[n2 * side + index],
            send_sem=s2_send.at[CORES * index + core],
            recv_sem=s2_recv.at[n2 * side + index],
            device_id=chip_dev(off2[index], side),
            device_id_type=MESH,
        )

    for index in range(n2):
        for side in sides(index, 0):
            push2(index, side).start()
    win2[n2 * core] = wide

    for half in range(2):
        gr_ref[0, :, LANES * half : LANES * (half + 1)] = (upstream(half) * conv_of(half)).astype(gr_ref.dtype)
    g_recv()
    for half in range(2):
        grad_mixed = recv_g[pl.ds(half, chans, stride=2), :] * fscale + gain * pulled_of(half)
        gr_ref[1, :, LANES * half : LANES * (half + 1)] = (grad_mixed * dequant(2, half)).astype(gr_ref.dtype)
        gr_ref[2, :, LANES * half : LANES * (half + 1)] = (grad_mixed * dequant(1, half)).astype(gr_ref.dtype)
    f_recv()
    reach = column(7)
    for half in range(2):
        lags = (me * (2 * LANES) + half * LANES + lax.broadcasted_iota(jnp.int32, (1, LANES), 1)).astype(jnp.float32)
        fg_ref[:, LANES * half : LANES * (half + 1)] = jnp.where(
            lags < reach, recv_f[pl.ds(half, chans, stride=2), :] * fscale, 0.0
        )

    for index in range(n2):
        for side in sides(index, 0):
            land2(index, side).wait_recv()
    for half in range(2):
        largest = jnp.max(win2[n2 * half : n2 * (half + 1)], axis=0)
        tm_ref[:, LANES * half : LANES * (half + 1)] = largest
        response = dequant(0, half) * conv_of(half)
        so_ref[:, LANES * half : LANES * (half + 1)] = (response / (largest + 1e-06)).astype(so_ref.dtype)

    for sent in (m_sent, p_sent, y_sent, g_sent, f_sent):
        sent()
    for index in range(n1):
        for side in sides(index, self1):
            push1(index, side).wait_send()
    for index in range(n2):
        for side in sides(index, 0):
            push2(index, side).wait_send()


def body(proj, scale_exp, filt, reach, skip, cotangent):
    groups, chans, span = proj.shape
    parts = lax.axis_size("ctx")
    chips = lax.axis_size("ch") // CORES
    seq = parts * span
    own = chans // parts
    divisors = jnp.array(REACH_DIVISORS, dtype=jnp.int32)
    class_ids = jnp.arange(len(REACH_DIVISORS), dtype=jnp.int32)
    reach_div = jnp.sum(jnp.where(reach[:, None] == class_ids[None, :], divisors[None, :], 0), axis=1)
    reach_len = seq // reach_div
    scaled = jnp.exp2(scale_exp.astype(jnp.float32))
    aux = jnp.concatenate(
        [jnp.transpose(scaled, (1, 0, 2)).reshape(chans, 2 * groups), skip[:, None], reach_len.astype(jnp.float32)[:, None]],
        axis=1,
    )
    n1, n2 = (len(offsets) for offsets in z_windows(chips))
    slab = pltpu.VMEM((2 * chans, LANES), jnp.float32)
    vmem = pl.BlockSpec(memory_space=pltpu.VMEM)
    scaled_out, token_max, gradients, filter_grad = pl.pallas_call(
        functools.partial(kernel, parts, chips, chans, seq),
        out_shape=(
            jax.ShapeDtypeStruct((chans, span), jnp.bfloat16),
            jax.ShapeDtypeStruct((1, span), jnp.float32),
            jax.ShapeDtypeStruct((groups, chans, span), jnp.bfloat16),
            jax.ShapeDtypeStruct((chans, span), jnp.float32),
        ),
        in_specs=[vmem, vmem, vmem, pl.BlockSpec(memory_space=pl.ANY)],
        out_specs=(vmem, vmem, vmem, vmem),
        scratch_shapes=[slab] * 10
        + [
            pltpu.VMEM((16, seq), jnp.bfloat16),
            pltpu.VMEM((16, seq), jnp.float32),
            pltpu.VMEM((own, 2 * LANES, seq), jnp.bfloat16),
            pltpu.VMEM((2, 2 * parts, LANES), jnp.float32),
            pltpu.VMEM((2 * parts, seq), jnp.bfloat16),
            slab,
            pltpu.VMEM((2, 1, LANES), jnp.float32),
            pltpu.VMEM((CORES * n1, 1, LANES), jnp.float32),
            pltpu.VMEM((1, 1, LANES), jnp.float32),
            pltpu.VMEM((CORES * n2, 1, LANES), jnp.float32),
            pltpu.SemaphoreType.DMA,
            pltpu.SemaphoreType.DMA((5, parts)),
            pltpu.SemaphoreType.DMA((5, parts)),
            pltpu.SemaphoreType.DMA((CORES * n1,)),
            pltpu.SemaphoreType.DMA((CORES * n1,)),
            pltpu.SemaphoreType.DMA((CORES * n2,)),
            pltpu.SemaphoreType.DMA((CORES * n2,)),
        ],
        compiler_params=pltpu.CompilerParams(
            collective_id=0, has_side_effects=True, vmem_limit_bytes=40 * 1024 * 1024
        ),
        name="hyena",
    )(aux, proj, cotangent, filt)
    return scaled_out, token_max.reshape(span), gradients, filter_grad


def solution(mesh):
    return jax.shard_map(
        body,
        mesh=mesh,
        in_specs=(
            P(None, "ch", "ctx"),
            P(None, "ch", "ctx"),
            P("ch", None),
            P("ch"),
            P("ch"),
            P("ch", "ctx"),
        ),
        out_specs=(P("ch", "ctx"), P("ctx"), P(None, "ch", "ctx"), P("ch", "ctx")),
        check_vma=False,
    )
```

time: 186 us -> 65.5 us (0.35)
  blocking collectives: 132 us -> 0 us
  Pallas kernels: 0 us -> 57.1 us
  other arithmetic: 17.8 us -> 2.23 us
  between operations: 14.2 us -> 0.67 us
  matrix products: 9.36 us -> 0 us
  waiting for transfers between devices: 5.14 us -> 0 us
  starting transfers between devices: 4.93 us -> 0 us
  local copies, waits for them, and re-layouts: 1.79 us -> 5.12 us
    pmax x1 -> x0, blocking collectives: 112 us -> none  [body(): token_max = lax.pmax(local_peak, 'ch')]
    pallas_call x0 -> x1, Pallas kernels: none -> 57.1 us  [body(): pl.pallas_call(functools.partial(kernel, parts, chips, chans, seq), out_s...]
    all_gather x1 -> x0, blocking collectives: 20.2 us -> none  [body(): shard_piece = lax.all_gather(pulled_bf, 'ctx', axis=1, tiled=True)]
    dot_general x6 -> x0, matrix products: 9.36 us -> none  [the longest x3 6.11 us: from_spectrum(): jnp.einsum('...f,sf->...s', spectrum, basis, precision=lax.Precision.HIGH...]
    add x5 -> x0, other arithmetic: 5.38 us -> none  [the longest x1 2.76 us: body(): near_plus = near_spec + rotate(next_spec, parity)]
    all_to_all x1 -> x0, waiting for transfers between devices: 5.13 us -> none  [body(): lax.all_to_all(pieces, 'ctx', split_axis=0, concat_axis=0, tiled=True)]
    unnamed x10 -> x12, local copies, waits for them, and re-layouts: 0.02 us -> 5.02 us
    all_to_all x1 -> x0, starting transfers between devices: 4.7 us -> none  [body(): lax.all_to_all(pieces, 'ctx', split_axis=0, concat_axis=0, tiled=True)]
  transfers between devices with their start and end apart: 2 -> 0, of which waited for: 1 -> 0; matrix products, arithmetic and copies ran while one was open for 5% -> 0% of each run, Pallas kernels for 0% -> 0%
where the time goes in v1:
time: 65.5 us; the launch traced here: 65.2 us
  Pallas kernels  57.1 us (87%)
  local copies, waits for them, and re-layouts  5.12 us (8%)
  other arithmetic  2.23 us (3%)
  between operations  0.67 us (1%)
    pallas_call x1, Pallas kernels, body(): pl.pallas_call(functools.partial(kernel, parts, chips, chans, seq), out_s...  57.1 us
    unnamed x12, local copies, waits for them, and re-layouts  5.02 us

profile of v1, /device:TPU:1, one launch (start us, length us, event | category | flops | bytes accessed | tf_op | source)
XLA Modules:
  0.0 65.2 jit_solution(4513280673998736131)
XLA Ops:
  0.6 0.0 copy-start.3
  0.6 0.0 copy-start.2
  0.7 0.6 copy-done.3
  1.3 0.7 %select_reduce_fusion = s32[64]{0:T(128)S(1)} fusion(s32[5]{0:T(128)S(1)} %copy-done.3, s32[64]{0:T(128)} %param.10), kind=kLoop, calls=%fused_computation.1 | loop fusion | flops 896 | bytes 532 | tf_op jit(solution)/shard_map/reduce_sum | solution.py:344
  2.0 0.1 fusion
  2.2 0.7 %exponential_bitcast_fusion = f32[64,3,2]{0,2,1:T(2,128)S(1)} fusion(s32[3,64,2]{1,2,0:T(2,128)} %param.8), kind=kLoop, calls=%fused_computation.3 | loop fusion | flops 768 | bytes 3072 | tf_op jit(solution)/shard_map/transpose | solution.py:348
  2.9 0.7 %pad_maximum_fusion = f32[64,8]{0,1:T(8,128)S(1)} fusion(f32[64,1]{0,1:T(1,128)S(1)} %fusion, f32[64,1]{0,1:T(1,128)} %bitcast.15, f32[64,6]{0,1:T(8,128)S(1)} %reshape.57), kind=kLoop, calls=%fused_computation | loop fusion | flops 1024 | bytes 4096 | tf_op jit(solution)/shard_map/concatenate | solution.py:347
  3.5 0.1 copy.22.aux
  3.6 0.0 copy-done.2
  3.6 0.0 copy-start
  3.6 1.0 %copy-done = bf16[64,4096]{1,0:T(8,128)(2,1)S(1)} copy-done((bf16[64,4096]{1,0:T(8,128)(2,1)S(1)}, bf16[64,4096]{1,0:T(8,128)(2,1)}, u32[]{:S(2)}) %copy-start) | copy-done | bytes 524312
  4.7 0.0 copy-start.1
  4.7 0.9 %copy-done.1 = bf16[3,64,256]{2,1,0:T(8,128)(2,1)S(1)} copy-done((bf16[3,64,256]{2,1,0:T(8,128)(2,1)S(1)}, bf16[3,64,256]{2,1,0:T(8,128)(2,1)}, u32[]{:S(2)}) %copy-start.1) | copy-done | bytes 98328
  5.6 57.1 %hyena.1 = (bf16[64,256]{1,0:T(8,128)(2,1)S(1)}, f32[1,256]{1,0:T(1,128)S(1)}, bf16[3,64,256]{2,1,0:T(8,128)(2,1)S(1)}, f32[64,256]{1,0:T(8,128)S(1)}) custom-call(f32[64,8]{1,0:T(8,128)S(1)} %copy.22.aux, bf16[3,64,256]{2,1,0:T(8,128)(2,1)S(1)} %copy-done.1, bf16[64,256]{1,0:T(8,128)(2,1)S(1)} %copy-done.2, bf16[64,4096]{1,0:T(8,128)(2,1)S(1)} %copy-done), custom_call_target="tpu_custom_call" | custom-call | tf_op jit(solution)/shard_map/hyena/pallas_call | solution.py:354
  62.7 0.6 copy.27
  63.3 0.6 copy.28
  63.9 0.6 copy.29
  64.5 0.6 copy.30
  (1 shorter events, 0.0 us)
Async XLA Ops:
  0.6 0.7 %copy-start.3 = (s32[5]{0:T(128)S(1)}, s32[5]{0:T(128)}, u32[]{:S(2)}) copy-start(s32[5]{0:T(128)} %constant.16.clone) | copy-start | bytes 64
  0.6 3.0 %copy-start.2 = (bf16[64,256]{1,0:T(8,128)(2,1)S(1)}, bf16[64,256]{1,0:T(8,128)(2,1)}, u32[]{:S(2)}) copy-start(bf16[64,256]{1,0:T(8,128)(2,1)} %cot.1) | copy-start | bytes 98308
  3.6 1.0 %copy-start = (bf16[64,4096]{1,0:T(8,128)(2,1)S(1)}, bf16[64,4096]{1,0:T(8,128)(2,1)}, u32[]{:S(2)}) copy-start(bf16[64,4096]{1,0:T(8,128)(2,1)} %filt.1) | copy-start | bytes 1572868
  4.7 0.9 %copy-start.1 = (bf16[3,64,256]{2,1,0:T(8,128)(2,1)S(1)}, bf16[3,64,256]{2,1,0:T(8,128)(2,1)}, u32[]{:S(2)}) copy-start(bf16[3,64,256]{2,1,0:T(8,128)(2,1)} %proj.1) | copy-start | bytes 294916

commit v2 on v1

--- a/solution.py
+++ b/solution.py
@@ -19,6 +19,12 @@
     if chips == 32:
         return tuple(range(-5, 6)), (0, -11, 11)
     return tuple(range(chips)), (0,)
+
+
+def z_greetings(chips):
+    if chips == 32:
+        return tuple(range(-3, 4)), (3, 6)
+    return tuple(range(chips)), ()
 
 
 def fine_shifts(row, dst):
@@ -36,13 +42,15 @@
 
 def kernel(
     parts, chips, chans, seq,
-    aux, proj, cot, filt,
+    proj_hbm, scale_hbm, cot_hbm, filt, reach_hbm, skip_hbm,
+    so_hbm, tm_hbm, gr_hbm, fg_hbm,
     so_ref, tm_ref, gr_ref, fg_ref,
     send_m, send_p, send_y, send_g, send_f,
     recv_m, recv_p, recv_y, recv_g, recv_f,
-    taps_bf, taps, fine, pads, left, rev,
+    proj, scale, cot, reach_row, skip_row, wide_rows, aux, response,
+    taps_bf, taps, fine, pads, left, rev, turned,
     lm, win1, wsend, win2,
-    taps_sem, ctx_send, ctx_recv, s1_send, s1_recv, s2_send, s2_recv,
+    in_sem, out_sem, ctx_send, ctx_recv, s1_send, s1_recv, s2_send, s2_recv, relay_sem,
 ):
     own = chans // parts
     rows = 2 * own
@@ -52,6 +60,7 @@
     zpos = ch // CORES
     core = ch % CORES
     off1, off2 = z_windows(chips)
+    near, relays = z_greetings(chips)
     n1, n2 = len(off1), len(off2)
     self1 = off1.index(0)
 
@@ -60,11 +69,6 @@
 
     def chip_dev(offset, side):
         return {"ch": lax.rem(zpos + (offset + chips), chips) * CORES + side}
-
-    per_tile = 16 // own
-    tile = pl.multiple_of(me // per_tile * 16, 16)
-    tap_copy = pltpu.make_async_copy(filt.at[pl.ds(tile, 16), :], taps_bf, taps_sem)
-    tap_copy.start()
 
     barrier = pltpu.get_barrier_semaphore()
 
@@ -74,14 +78,47 @@
 
     lax.fori_loop(1, parts, greet, 0)
     greeted = parts - 1
-    for offset in off1 + off2[1:]:
-        if offset == 0:
-            pl.semaphore_signal(barrier, inc=1, device_id=chip_dev(0, 1 - core), device_id_type=MESH)
+    for offset in near:
+        for side in (1 - core,) if offset == 0 else tuple(range(CORES)):
+            pl.semaphore_signal(barrier, inc=1, device_id=chip_dev(offset, side), device_id_type=MESH)
             greeted += 1
-        else:
-            for side in range(CORES):
-                pl.semaphore_signal(barrier, inc=1, device_id=chip_dev(offset, side), device_id_type=MESH)
-                greeted += 1
+
+    def relay_send(index):
+        for offset in (-relays[index], relays[index]):
+            pl.semaphore_signal(relay_sem.at[index], inc=1, device_id=chip_dev(offset, core), device_id_type=MESH)
+
+    def relay_wait(index):
+        pl.semaphore_wait(relay_sem.at[index], 2)
+
+    per_tile = 16 // own
+    tile = pl.multiple_of(me // per_tile * 16, 16)
+    fetches = [
+        pltpu.make_async_copy(src, dst, in_sem.at[index])
+        for index, (src, dst) in enumerate(
+            (
+                (proj_hbm, proj),
+                (scale_hbm, scale),
+                (cot_hbm, cot),
+                (reach_hbm, reach_row),
+                (skip_hbm, skip_row),
+                (filt.at[pl.ds(tile, 16), :], taps_bf),
+            )
+        )
+    ]
+    for fetch in fetches:
+        fetch.start()
+    for fetch in fetches[:-1]:
+        fetch.wait()
+
+    wide_rows[...] = jnp.zeros_like(wide_rows)
+    for group in range(3):
+        wide_rows[2 * group : 2 * group + 2, 0:chans] = jnp.exp2(scale[group].astype(jnp.float32))
+    wide_rows[6:7, 0:chans] = skip_row[...]
+    reach_len = jnp.zeros((1, chans), jnp.float32)
+    for index, divisor in enumerate(REACH_DIVISORS):
+        reach_len = jnp.where(reach_row[...] == index, float(seq // divisor), reach_len)
+    wide_rows[7:8, 0:chans] = reach_len
+    aux[...] = jnp.transpose(wide_rows[...])[0:chans]
 
     def column(index):
         return aux[:, index : index + 1]
@@ -160,9 +197,11 @@
 
     pl.semaphore_wait(barrier, greeted)
     m_start()
+    if relays:
+        relay_send(0)
     p_start()
 
-    tap_copy.wait()
+    fetches[-1].wait()
     taps[...] = taps_bf[...].astype(jnp.float32)
     lag = lax.broadcasted_iota(jnp.int32, (1, seq), 1).astype(jnp.float32)
     for j in range(own):
@@ -191,16 +230,21 @@
             at = parts - n // 2
             block = pads[n % 2, at : at + parts, :].astype(jnp.bfloat16)
             if n < 2 * parts:
-                left[0:parts, LANES * n : LANES * (n + 1)] = block
+                left[j, 0:parts, LANES * n : LANES * (n + 1)] = block
             if n >= 1:
-                left[parts : 2 * parts, LANES * (n - 1) : LANES * n] = block
-        out = lax.dot_general(left[...], fine[j, 0:LANES, :], NT, preferred_element_type=jnp.float32)
-        top = out.astype(jnp.bfloat16)
-        rest = (out - top.astype(jnp.float32)).astype(jnp.bfloat16)
-        back = reverse(top) + reverse(rest)
-        send_y[pl.ds(2 * j, parts, stride=rows), :] = back[parts:]
-        send_y[pl.ds(2 * j + 1, parts, stride=rows), :] = back[:parts]
+                left[j, parts : 2 * parts, LANES * (n - 1) : LANES * n] = block
+    for j in range(own):
+        out = lax.dot_general(left[j], fine[j, 0:LANES, :], NT, preferred_element_type=jnp.float32)
+        turned[pl.ds(2 * j, parts, stride=rows), :] = out[parts:]
+        turned[pl.ds(2 * j + 1, parts, stride=rows), :] = out[:parts]
+    whole = turned[...]
+    top = whole.astype(jnp.bfloat16)
+    rest = (whole - top.astype(jnp.float32)).astype(jnp.bfloat16)
+    send_y[...] = reverse(top) + reverse(rest)
     y_start()
+    if relays:
+        relay_wait(0)
+        relay_send(1)
 
     def gradients_of(j):
         blocks = [recv_m[rows * c + 2 * j + half : rows * c + 2 * j + half + 1, :] for c in range(parts) for half in range(2)]
@@ -212,17 +256,17 @@
             at = n // 2
             block = pads[n % 2, at : at + parts, :].astype(jnp.bfloat16)
             if n < 2 * parts:
-                left[0:parts, LANES * n : LANES * (n + 1)] = block
+                left[j, 0:parts, LANES * n : LANES * (n + 1)] = block
             if n >= 1:
-                left[parts : 2 * parts, LANES * (n - 1) : LANES * n] = block
-        out = lax.dot_general(left[...], fine[j], NT, preferred_element_type=jnp.float32)
+                left[j, parts : 2 * parts, LANES * (n - 1) : LANES * n] = block
+        out = lax.dot_general(left[j], fine[j], NT, preferred_element_type=jnp.float32)
         for half in range(2):
             part = out[parts * half : parts * (half + 1)]
             send_g[pl.ds(2 * j + half, parts, stride=rows), :] = part[:, :LANES]
             send_f[pl.ds(2 * j + half, parts, stride=rows), :] = part[:, LANES:]
 
     p_recv()
-    for j in range(own // 2):
+    for j in range(own):
         gradients_of(j)
 
     y_recv()
@@ -232,8 +276,9 @@
         return recv_y[pl.ds(half, chans, stride=2), :] * fscale + gain * mixed_of(half)
 
     for half in range(2):
-        peak = jnp.max(jnp.abs(dequant(0, half) * conv_of(half)), axis=0, keepdims=True)
-        lm[half] = peak
+        value = dequant(0, half) * conv_of(half)
+        response[:, LANES * half : LANES * (half + 1)] = value
+        lm[half] = jnp.max(jnp.abs(value), axis=0, keepdims=True)
 
     def push1(index, side):
         return pltpu.make_async_remote_copy(
@@ -263,8 +308,6 @@
             push1(index, side).start()
     win1[CORES * self1 + core] = lm[core]
 
-    for j in range(own // 2, own):
-        gradients_of(j)
     g_start()
     f_start()
 
@@ -273,6 +316,8 @@
             land1(index, side).wait_recv()
     wide = jnp.max(win1[...], axis=0)
     wsend[0] = wide
+    if relays:
+        relay_wait(1)
 
     def push2(index, side):
         return pltpu.make_async_remote_copy(
@@ -299,6 +344,12 @@
             push2(index, side).start()
     win2[n2 * core] = wide
 
+    stores = [
+        pltpu.make_async_copy(src, dst, out_sem.at[index])
+        for index, (src, dst) in enumerate(
+            ((gr_ref, gr_hbm), (fg_ref, fg_hbm), (tm_ref, tm_hbm), (so_ref, so_hbm))
+        )
+    ]
     for half in range(2):
         gr_ref[0, :, LANES * half : LANES * (half + 1)] = (upstream(half) * conv_of(half)).astype(gr_ref.dtype)
     g_recv()
@@ -306,6 +357,7 @@
         grad_mixed = recv_g[pl.ds(half, chans, stride=2), :] * fscale + gain * pulled_of(half)
         gr_ref[1, :, LANES * half : LANES * (half + 1)] = (grad_mixed * dequant(2, half)).astype(gr_ref.dtype)
         gr_ref[2, :, LANES * half : LANES * (half + 1)] = (grad_mixed * dequant(1, half)).astype(gr_ref.dtype)
+    stores[0].start()
     f_recv()
     reach = column(7)
     for half in range(2):
@@ -314,14 +366,19 @@
             lags < reach, recv_f[pl.ds(half, chans, stride=2), :] * fscale, 0.0
         )
 
+    stores[1].start()
+
     for index in range(n2):
         for side in sides(index, 0):
             land2(index, side).wait_recv()
     for half in range(2):
         largest = jnp.max(win2[n2 * half : n2 * (half + 1)], axis=0)
         tm_ref[:, LANES * half : LANES * (half + 1)] = largest
-        response = dequant(0, half) * conv_of(half)
-        so_ref[:, LANES * half : LANES * (half + 1)] = (response / (largest + 1e-06)).astype(so_ref.dtype)
+        value = response[:, LANES * half : LANES * (half + 1)]
+        so_ref[:, LANES * half : LANES * (half + 1)] = (value / (largest + 1e-06)).astype(so_ref.dtype)
+
+    stores[2].start()
+    stores[3].start()
 
     for sent in (m_sent, p_sent, y_sent, g_sent, f_sent):
         sent()
@@ -331,6 +388,18 @@
     for index in range(n2):
         for side in sides(index, 0):
             push2(index, side).wait_send()
+    for store in stores:
+        store.wait()
+
+
+def write_out(*refs):
+    count = len(refs) // 2
+    sems = refs[-1]
+    copies = [pltpu.make_async_copy(refs[index], refs[count + index], sems.at[index]) for index in range(count)]
+    for copy in copies:
+        copy.start()
+    for copy in copies:
+        copy.wait()
 
 
 def body(proj, scale_exp, filt, reach, skip, cotangent):
@@ -339,53 +408,72 @@
     chips = lax.axis_size("ch") // CORES
     seq = parts * span
     own = chans // parts
-    divisors = jnp.array(REACH_DIVISORS, dtype=jnp.int32)
-    class_ids = jnp.arange(len(REACH_DIVISORS), dtype=jnp.int32)
-    reach_div = jnp.sum(jnp.where(reach[:, None] == class_ids[None, :], divisors[None, :], 0), axis=1)
-    reach_len = seq // reach_div
-    scaled = jnp.exp2(scale_exp.astype(jnp.float32))
-    aux = jnp.concatenate(
-        [jnp.transpose(scaled, (1, 0, 2)).reshape(chans, 2 * groups), skip[:, None], reach_len.astype(jnp.float32)[:, None]],
-        axis=1,
-    )
     n1, n2 = (len(offsets) for offsets in z_windows(chips))
     slab = pltpu.VMEM((2 * chans, LANES), jnp.float32)
-    vmem = pl.BlockSpec(memory_space=pltpu.VMEM)
-    scaled_out, token_max, gradients, filter_grad = pl.pallas_call(
+    hbm = pl.BlockSpec(memory_space=pltpu.HBM)
+    shapes = (
+        jax.ShapeDtypeStruct((chans, span), jnp.bfloat16),
+        jax.ShapeDtypeStruct((1, span), jnp.float32),
+        jax.ShapeDtypeStruct((groups, chans, span), jnp.bfloat16),
+        jax.ShapeDtypeStruct((chans, span), jnp.float32),
+    )
+    results = pl.pallas_call(
         functools.partial(kernel, parts, chips, chans, seq),
-        out_shape=(
-            jax.ShapeDtypeStruct((chans, span), jnp.bfloat16),
-            jax.ShapeDtypeStruct((1, span), jnp.float32),
-            jax.ShapeDtypeStruct((groups, chans, span), jnp.bfloat16),
-            jax.ShapeDtypeStruct((chans, span), jnp.float32),
-        ),
-        in_specs=[vmem, vmem, vmem, pl.BlockSpec(memory_space=pl.ANY)],
-        out_specs=(vmem, vmem, vmem, vmem),
-        scratch_shapes=[slab] * 10
+        out_shape=shapes,
+        in_specs=[hbm] * 6,
+        out_specs=(hbm,) * 4,
+        scratch_shapes=[pltpu.VMEM(shape.shape, shape.dtype) for shape in shapes]
+        + [slab] * 10
         + [
+            pltpu.VMEM((groups, chans, span), jnp.bfloat16),
+            pltpu.VMEM((groups, 2, chans), jnp.int32),
+            pltpu.VMEM((chans, span), jnp.bfloat16),
+            pltpu.VMEM((1, chans), jnp.int32),
+            pltpu.VMEM((1, chans), jnp.float32),
+            pltpu.VMEM((8, LANES), jnp.float32),
+            pltpu.VMEM((chans, 8), jnp.float32),
+            pltpu.VMEM((chans, span), jnp.float32),
             pltpu.VMEM((16, seq), jnp.bfloat16),
             pltpu.VMEM((16, seq), jnp.float32),
             pltpu.VMEM((own, 2 * LANES, seq), jnp.bfloat16),
             pltpu.VMEM((2, 2 * parts, LANES), jnp.float32),
-            pltpu.VMEM((2 * parts, seq), jnp.bfloat16),
+            pltpu.VMEM((own, 2 * parts, seq), jnp.bfloat16),
+            slab,
             slab,
             pltpu.VMEM((2, 1, LANES), jnp.float32),
             pltpu.VMEM((CORES * n1, 1, LANES), jnp.float32),
             pltpu.VMEM((1, 1, LANES), jnp.float32),
             pltpu.VMEM((CORES * n2, 1, LANES), jnp.float32),
-            pltpu.SemaphoreType.DMA,
+            pltpu.SemaphoreType.DMA((6,)),
+            pltpu.SemaphoreType.DMA((4,)),
             pltpu.SemaphoreType.DMA((5, parts)),
             pltpu.SemaphoreType.DMA((5, parts)),
             pltpu.SemaphoreType.DMA((CORES * n1,)),
             pltpu.SemaphoreType.DMA((CORES * n1,)),
             pltpu.SemaphoreType.DMA((CORES * n2,)),
             pltpu.SemaphoreType.DMA((CORES * n2,)),
+            pltpu.SemaphoreType.REGULAR((2,)),
         ],
         compiler_params=pltpu.CompilerParams(
-            collective_id=0, has_side_effects=True, vmem_limit_bytes=40 * 1024 * 1024
+            collective_id=0, has_side_effects=True, vmem_limit_bytes=58 * 1024 * 1024
         ),
         name="hyena",
-    )(aux, proj, cotangent, filt)
+    )(
+        proj,
+        jnp.transpose(scale_exp, (0, 2, 1)),
+        cotangent,
+        filt,
+        reach.reshape(1, chans),
+        skip.reshape(1, chans),
+    )
+    scaled_out, token_max, gradients, filter_grad = pl.pallas_call(
+        write_out,
+        out_shape=shapes,
+        in_specs=[pl.BlockSpec(memory_space=pl.ANY)] * 4,
+        out_specs=(hbm,) * 4,
+        scratch_shapes=[pltpu.SemaphoreType.DMA((4,))],
+        name="write_out",
+    )(*results)
     return scaled_out, token_max.reshape(span), gradients, filter_grad
 
 

time: 65.5 us -> 60.6 us (0.925)
  local copies, waits for them, and re-layouts: 5.12 us -> 0 us
  Pallas kernels: 57.1 us -> 59.8 us
  other arithmetic: 2.23 us -> 0 us
    pallas_call x0 -> x1, Pallas kernels: none -> 7.13 us  [body(): pl.pallas_call(write_out, out_shape=shapes, in_specs=[pl.BlockSpec(memory...]
    unnamed x12 -> x0, local copies, waits for them, and re-layouts: 5.02 us -> none
    pallas_call x1, Pallas kernels: 57.1 us -> 52.7 us  [body(): pl.pallas_call(functools.partial(kernel, parts, chips, chans, seq), out_s...]
    reduce_sum x1 -> x0, other arithmetic: 0.74 us -> none  [body(): jnp.sum(jnp.where(reach[:, None] == class_ids[None, :], divisors[None, :]...]
    transpose x1 -> x0, other arithmetic: 0.69 us -> none  [body(): jnp.transpose(scaled, (1, 0, 2)).reshape(chans, 2 * groups)]
    concatenate x1 -> x0, other arithmetic: 0.67 us -> none  [body(): jnp.concatenate([jnp.transpose(scaled, (1, 0, 2)).reshape(chans, 2 * grou...]
where the time goes in v2:
time: 60.6 us; the launch traced here: 60.5 us
  Pallas kernels  59.8 us (99%)
  between operations  0.64 us (1%)
    pallas_call x1, Pallas kernels, body(): pl.pallas_call(functools.partial(kernel, parts, chips, chans, seq), out_s...  52.7 us
    pallas_call x1, Pallas kernels, body(): pl.pallas_call(write_out, out_shape=shapes, in_specs=[pl.BlockSpec(memory...  7.13 us

profile of v2, /device:TPU:1, one launch (start us, length us, event | category | flops | bytes accessed | tf_op | source)
XLA Modules:
  0.0 60.5 jit_solution(13719964398798537892)
XLA Ops:
  0.6 52.7 %hyena.1 = (bf16[64,256]{1,0:T(8,128)(2,1)}, f32[1,256]{1,0:T(1,128)}, bf16[3,64,256]{2,1,0:T(8,128)(2,1)}, f32[64,256]{1,0:T(8,128)}) custom-call(bf16[3,64,256]{2,1,0:T(8,128)(2,1)} %proj_hbm.1, s32[3,2,64]{2,1,0:T(2,128)} %bitcast.4, bf16[64,256]{1,0:T(8,128)(2,1)} %cot_hbm.1, bf16[64,4096]{1,0:T(8,128)(2,1)} %filt.1, s32[1,64]{1,0:T(1,128)} %bitcast.5, ...), custom_call_target="tpu_custom_call" | custom-call | tf_op jit(solution)/shard_map/hyena/pallas_call | solution.py:420
  53.3 7.1 %write_out.1 = (bf16[64,256]{1,0:T(8,128)(2,1)}, f32[1,256]{1,0:T(1,128)}, bf16[3,64,256]{2,1,0:T(8,128)(2,1)}, f32[64,256]{1,0:T(8,128)}) custom-call(bf16[64,256]{1,0:T(8,128)(2,1)} %get-tuple-element.12.refs_0_, f32[1,256]{1,0:T(1,128)} %get-tuple-element.13.refs_1_, bf16[3,64,256]{2,1,0:T(8,128)(2,1)} %get-tuple-element.14.refs_2_, ...), custom_call_target="tpu_custom_call" | custom-call | tf_op jit(solution)/shard_map/write_out/pallas_call | solution.py:469

commit v3 on v2

--- a/solution.py
+++ b/solution.py
@@ -15,16 +15,18 @@
 NT = (((1,), (1,)), ((), ()))
 
 
-def z_windows(chips):
-    if chips == 32:
-        return tuple(range(-5, 6)), (0, -11, 11)
-    return tuple(range(chips)), (0,)
-
-
 def z_greetings(chips):
     if chips == 32:
-        return tuple(range(-3, 4)), (3, 6)
+        return tuple(range(-4, 5)), (4, 8)
     return tuple(range(chips)), ()
+
+
+def ctx_offsets(parts):
+    if parts != 16:
+        return None
+    def hops(offset):
+        return sum(min(part, 4 - part) for part in offset)
+    return sorted(((a, b) for a in range(4) for b in range(4) if a or b), key=lambda offset: -hops(offset))
 
 
 def fine_shifts(row, dst):
@@ -43,14 +45,13 @@
 def kernel(
     parts, chips, chans, seq,
     proj_hbm, scale_hbm, cot_hbm, filt, reach_hbm, skip_hbm,
-    so_hbm, tm_hbm, gr_hbm, fg_hbm,
     so_ref, tm_ref, gr_ref, fg_ref,
     send_m, send_p, send_y, send_g, send_f,
     recv_m, recv_p, recv_y, recv_g, recv_f,
     proj, scale, cot, reach_row, skip_row, wide_rows, aux, response,
     taps_bf, taps, fine, pads, left, rev, turned,
-    lm, win1, wsend, win2,
-    in_sem, out_sem, ctx_send, ctx_recv, s1_send, s1_recv, s2_send, s2_recv, relay_sem,
+    lm, win, wide, other,
+    in_sem, ctx_send, ctx_recv, z_send, z_recv, core_sem, relay_sem,
 ):
     own = chans // parts
     rows = 2 * own
@@ -59,10 +60,7 @@
     ch = lax.axis_index("ch")
     zpos = ch // CORES
     core = ch % CORES
-    off1, off2 = z_windows(chips)
     near, relays = z_greetings(chips)
-    n1, n2 = len(off1), len(off2)
-    self1 = off1.index(0)
 
     def peer_of(step):
         return lax.rem(me + step, parts)
@@ -72,11 +70,13 @@
 
     barrier = pltpu.get_barrier_semaphore()
 
-    def greet(step, carry):
-        pl.semaphore_signal(barrier, inc=1, device_id={"ctx": peer_of(step)}, device_id_type=MESH)
-        return carry
-
-    lax.fori_loop(1, parts, greet, 0)
+    offsets = ctx_offsets(parts)
+    if offsets is None:
+        far_first = [peer_of(step) for step in range(1, parts)]
+    else:
+        far_first = [lax.rem(me // 4 + a, 4) * 4 + lax.rem(me % 4 + b, 4) for a, b in offsets]
+    for peer in far_first:
+        pl.semaphore_signal(barrier, inc=1, device_id={"ctx": peer}, device_id_type=MESH)
     greeted = parts - 1
     for offset in near:
         for side in (1 - core,) if offset == 0 else tuple(range(CORES)):
@@ -142,9 +142,8 @@
 
     mine = pl.ds(pl.multiple_of(rows * me, rows), rows)
 
-    def exchange(which, src, dst):
-        def copy(step):
-            peer = peer_of(step)
+    def exchange(which, src, dst, urgent=False):
+        def copy(peer):
             return pltpu.make_async_remote_copy(
                 src_ref=src.at[pl.ds(pl.multiple_of(rows * peer, rows), rows), :],
                 dst_ref=dst.at[mine, :],
@@ -167,10 +166,14 @@
 
         def start():
             def go(step, carry):
-                copy(step).start()
+                copy(peer_of(step)).start()
                 return carry
 
-            lax.fori_loop(1, parts, go, 0)
+            if urgent:
+                for peer in far_first:
+                    copy(peer).start()
+            else:
+                lax.fori_loop(1, parts, go, 0)
             dst[mine, :] = src[mine, :]
 
         def wait_recv():
@@ -182,16 +185,16 @@
 
         def wait_send():
             def go(step, carry):
-                copy(step).wait_send()
+                copy(peer_of(step)).wait_send()
                 return carry
 
             lax.fori_loop(1, parts, go, 0)
 
         return start, wait_recv, wait_send
 
-    m_start, m_recv, m_sent = exchange(0, send_m, recv_m)
+    m_start, m_recv, m_sent = exchange(0, send_m, recv_m, urgent=True)
     p_start, p_recv, p_sent = exchange(1, send_p, recv_p)
-    y_start, y_recv, y_sent = exchange(2, send_y, recv_y)
+    y_start, y_recv, y_sent = exchange(2, send_y, recv_y, urgent=True)
     g_start, g_recv, g_sent = exchange(3, send_g, recv_g)
     f_start, f_recv, f_sent = exchange(4, send_f, recv_f)
 
@@ -219,6 +222,9 @@
         return jnp.dot(values, flip, preferred_element_type=jnp.float32)
 
     m_recv()
+    if relays:
+        relay_wait(0)
+        relay_send(1)
     rev[...] = reverse(recv_m[...].astype(jnp.bfloat16))
     zeros = jnp.zeros((parts, LANES), jnp.float32)
     for slot in range(2):
@@ -242,9 +248,6 @@
     rest = (whole - top.astype(jnp.float32)).astype(jnp.bfloat16)
     send_y[...] = reverse(top) + reverse(rest)
     y_start()
-    if relays:
-        relay_wait(0)
-        relay_send(1)
 
     def gradients_of(j):
         blocks = [recv_m[rows * c + 2 * j + half : rows * c + 2 * j + half + 1, :] for c in range(parts) for half in range(2)]
@@ -278,78 +281,51 @@
     for half in range(2):
         value = dequant(0, half) * conv_of(half)
         response[:, LANES * half : LANES * (half + 1)] = value
-        lm[half] = jnp.max(jnp.abs(value), axis=0, keepdims=True)
-
-    def push1(index, side):
+        lm[0, :, LANES * half : LANES * (half + 1)] = jnp.max(jnp.abs(value), axis=0, keepdims=True)
+
+    def z_step(index):
+        return chips // 2 + (index + 1) // 2 * (1 - 2 * (index % 2))
+
+    def z_push(step):
         return pltpu.make_async_remote_copy(
-            src_ref=lm.at[side],
-            dst_ref=win1.at[CORES * index + core],
-            send_sem=s1_send.at[CORES * index + side],
-            recv_sem=s1_recv.at[CORES * index + core],
-            device_id=chip_dev(off1[index], side),
+            src_ref=lm.at[0],
+            dst_ref=win.at[zpos],
+            send_sem=z_send.at[step],
+            recv_sem=z_recv.at[zpos],
+            device_id=chip_dev(step, core),
             device_id_type=MESH,
         )
 
-    def land1(index, side):
+    def z_land(step):
+        origin = lax.rem(zpos + step, chips)
         return pltpu.make_async_remote_copy(
-            src_ref=lm.at[core],
-            dst_ref=win1.at[CORES * index + side],
-            send_sem=s1_send.at[CORES * index + core],
-            recv_sem=s1_recv.at[CORES * index + side],
-            device_id=chip_dev(off1[index], side),
+            src_ref=lm.at[0],
+            dst_ref=win.at[origin],
+            send_sem=z_send.at[step],
+            recv_sem=z_recv.at[origin],
+            device_id=chip_dev(step, core),
             device_id_type=MESH,
         )
 
-    def sides(index, home):
-        return (1 - core,) if index == home else tuple(range(CORES))
-
-    for index in range(n1):
-        for side in sides(index, self1):
-            push1(index, side).start()
-    win1[CORES * self1 + core] = lm[core]
-
+    def z_start(index, carry):
+        z_push(z_step(index)).start()
+        return carry
+
+    def z_arrive(index, carry):
+        z_land(z_step(chips - 2 - index)).wait_recv()
+        return carry
+
+    def z_sent(index, carry):
+        z_push(z_step(index)).wait_send()
+        return carry
+
+    if relays:
+        relay_wait(1)
+    lax.fori_loop(0, chips - 1, z_start, 0)
+    win[zpos] = lm[0]
     g_start()
     f_start()
 
-    for index in range(n1):
-        for side in sides(index, self1):
-            land1(index, side).wait_recv()
-    wide = jnp.max(win1[...], axis=0)
-    wsend[0] = wide
-    if relays:
-        relay_wait(1)
-
-    def push2(index, side):
-        return pltpu.make_async_remote_copy(
-            src_ref=wsend.at[0],
-            dst_ref=win2.at[n2 * core + index],
-            send_sem=s2_send.at[CORES * index + side],
-            recv_sem=s2_recv.at[n2 * core + index],
-            device_id=chip_dev(off2[index], side),
-            device_id_type=MESH,
-        )
-
-    def land2(index, side):
-        return pltpu.make_async_remote_copy(
-            src_ref=wsend.at[0],
-            dst_ref=win2.at[n2 * side + index],
-            send_sem=s2_send.at[CORES * index + core],
-            recv_sem=s2_recv.at[n2 * side + index],
-            device_id=chip_dev(off2[index], side),
-            device_id_type=MESH,
-        )
-
-    for index in range(n2):
-        for side in sides(index, 0):
-            push2(index, side).start()
-    win2[n2 * core] = wide
-
-    stores = [
-        pltpu.make_async_copy(src, dst, out_sem.at[index])
-        for index, (src, dst) in enumerate(
-            ((gr_ref, gr_hbm), (fg_ref, fg_hbm), (tm_ref, tm_hbm), (so_ref, so_hbm))
-        )
-    ]
     for half in range(2):
         gr_ref[0, :, LANES * half : LANES * (half + 1)] = (upstream(half) * conv_of(half)).astype(gr_ref.dtype)
     g_recv()
@@ -357,7 +333,6 @@
         grad_mixed = recv_g[pl.ds(half, chans, stride=2), :] * fscale + gain * pulled_of(half)
         gr_ref[1, :, LANES * half : LANES * (half + 1)] = (grad_mixed * dequant(2, half)).astype(gr_ref.dtype)
         gr_ref[2, :, LANES * half : LANES * (half + 1)] = (grad_mixed * dequant(1, half)).astype(gr_ref.dtype)
-    stores[0].start()
     f_recv()
     reach = column(7)
     for half in range(2):
@@ -366,30 +341,27 @@
             lags < reach, recv_f[pl.ds(half, chans, stride=2), :] * fscale, 0.0
         )
 
-    stores[1].start()
-
-    for index in range(n2):
-        for side in sides(index, 0):
-            land2(index, side).wait_recv()
-    for half in range(2):
-        largest = jnp.max(win2[n2 * half : n2 * (half + 1)], axis=0)
-        tm_ref[:, LANES * half : LANES * (half + 1)] = largest
-        value = response[:, LANES * half : LANES * (half + 1)]
-        so_ref[:, LANES * half : LANES * (half + 1)] = (value / (largest + 1e-06)).astype(so_ref.dtype)
-
-    stores[2].start()
-    stores[3].start()
+
+    lax.fori_loop(0, chips - 1, z_arrive, 0)
+    wide[0] = jnp.max(win[...], axis=0)
+    swap = pltpu.make_async_remote_copy(
+        src_ref=wide.at[0],
+        dst_ref=other.at[0],
+        send_sem=core_sem.at[0],
+        recv_sem=core_sem.at[1],
+        device_id=chip_dev(0, 1 - core),
+        device_id_type=MESH,
+    )
+    swap.start()
+    swap.wait_recv()
+    largest = jnp.maximum(wide[0], other[0])
+    tm_ref[...] = largest
+    so_ref[...] = (response[...] / (largest + 1e-06)).astype(so_ref.dtype)
 
     for sent in (m_sent, p_sent, y_sent, g_sent, f_sent):
         sent()
-    for index in range(n1):
-        for side in sides(index, self1):
-            push1(index, side).wait_send()
-    for index in range(n2):
-        for side in sides(index, 0):
-            push2(index, side).wait_send()
-    for store in stores:
-        store.wait()
+    lax.fori_loop(0, chips - 1, z_sent, 0)
+    swap.wait_send()
 
 
 def write_out(*refs):
@@ -408,9 +380,9 @@
     chips = lax.axis_size("ch") // CORES
     seq = parts * span
     own = chans // parts
-    n1, n2 = (len(offsets) for offsets in z_windows(chips))
     slab = pltpu.VMEM((2 * chans, LANES), jnp.float32)
     hbm = pl.BlockSpec(memory_space=pltpu.HBM)
+    vmem = pl.BlockSpec(memory_space=pltpu.VMEM)
     shapes = (
         jax.ShapeDtypeStruct((chans, span), jnp.bfloat16),
         jax.ShapeDtypeStruct((1, span), jnp.float32),
@@ -421,9 +393,8 @@
         functools.partial(kernel, parts, chips, chans, seq),
         out_shape=shapes,
         in_specs=[hbm] * 6,
-        out_specs=(hbm,) * 4,
-        scratch_shapes=[pltpu.VMEM(shape.shape, shape.dtype) for shape in shapes]
-        + [slab] * 10
+        out_specs=(vmem,) * 4,
+        scratch_shapes=[slab] * 10
         + [
             pltpu.VMEM((groups, chans, span), jnp.bfloat16),
             pltpu.VMEM((groups, 2, chans), jnp.int32),
@@ -440,31 +411,34 @@
             pltpu.VMEM((own, 2 * parts, seq), jnp.bfloat16),
             slab,
             slab,
-            pltpu.VMEM((2, 1, LANES), jnp.float32),
-            pltpu.VMEM((CORES * n1, 1, LANES), jnp.float32),
-            pltpu.VMEM((1, 1, LANES), jnp.float32),
-            pltpu.VMEM((CORES * n2, 1, LANES), jnp.float32),
+            pltpu.VMEM((1, 1, span), jnp.float32),
+            pltpu.VMEM((chips, 1, span), jnp.float32),
+            pltpu.VMEM((1, 1, span), jnp.float32),
+            pltpu.VMEM((1, 1, span), jnp.float32),
             pltpu.SemaphoreType.DMA((6,)),
-            pltpu.SemaphoreType.DMA((4,)),
             pltpu.SemaphoreType.DMA((5, parts)),
             pltpu.SemaphoreType.DMA((5, parts)),
-            pltpu.SemaphoreType.DMA((CORES * n1,)),
-            pltpu.SemaphoreType.DMA((CORES * n1,)),
-            pltpu.SemaphoreType.DMA((CORES * n2,)),
-            pltpu.SemaphoreType.DMA((CORES * n2,)),
+            pltpu.SemaphoreType.DMA((chips,)),
+            pltpu.SemaphoreType.DMA((chips,)),
+            pltpu.SemaphoreType.DMA((2,)),
             pltpu.SemaphoreType.REGULAR((2,)),
         ],
         compiler_params=pltpu.CompilerParams(
-            collective_id=0, has_side_effects=True, vmem_limit_bytes=58 * 1024 * 1024
+            collective_id=0, has_side_effects=True, vmem_limit_bytes=40 * 1024 * 1024
         ),
         name="hyena",
     )(
-        proj,
-        jnp.transpose(scale_exp, (0, 2, 1)),
-        cotangent,
-        filt,
-        reach.reshape(1, chans),
-        skip.reshape(1, chans),
+        *(
+            pltpu.with_memory_space_constraint(arg, pltpu.HBM)
+            for arg in (
+                proj,
+                jnp.transpose(scale_exp, (0, 2, 1)),
+                cotangent,
+                filt,
+                reach.reshape(1, chans),
+                skip.reshape(1, chans),
+            )
+        )
     )
     scaled_out, token_max, gradients, filter_grad = pl.pallas_call(
         write_out,
@@ -472,6 +446,7 @@
         in_specs=[pl.BlockSpec(memory_space=pl.ANY)] * 4,
         out_specs=(hbm,) * 4,
         scratch_shapes=[pltpu.SemaphoreType.DMA((4,))],
+        compiler_params=pltpu.CompilerParams(vmem_limit_bytes=1024 * 1024),
         name="write_out",
     )(*results)
     return scaled_out, token_max.reshape(span), gradients, filter_grad

time: 60.6 us -> 53.4 us (0.88)
  Pallas kernels: 59.8 us -> 52.6 us
    pallas_call x1, Pallas kernels: 7.13 us -> 0.71 us  [body(): pl.pallas_call(write_out, out_shape=shapes, in_specs=[pl.BlockSpec(memory...]
    pallas_call x1, Pallas kernels: 52.7 us -> 51.9 us  [body(): pl.pallas_call(functools.partial(kernel, parts, chips, chans, seq), out_s...]
where the time goes in v3:
time: 53.4 us; the launch traced here: 53.3 us
  Pallas kernels  52.6 us (99%)
  between operations  0.64 us (1%)
    pallas_call x1, Pallas kernels, body(): pl.pallas_call(functools.partial(kernel, parts, chips, chans, seq), out_s...  51.9 us

profile of v3, /device:TPU:1, one launch (start us, length us, event | category | flops | bytes accessed | tf_op | source)
XLA Modules:
  0.0 53.3 jit_solution(7679965059799485503)
XLA Ops:
  0.6 51.9 %hyena.1 = (bf16[64,256]{1,0:T(8,128)(2,1)S(1)}, f32[1,256]{1,0:T(1,128)S(1)}, bf16[3,64,256]{2,1,0:T(8,128)(2,1)S(1)}, f32[64,256]{1,0:T(8,128)S(1)}) custom-call(bf16[3,64,256]{2,1,0:T(8,128)(2,1)} %proj_hbm.1, s32[3,2,64]{2,1,0:T(2,128)} %bitcast.4, bf16[64,256]{1,0:T(8,128)(2,1)} %cot_hbm.1, bf16[64,4096]{1,0:T(8,128)(2,1)} %filt.1, s32[1,64]{1,0:T(1,128)} %bitcast.5, ...), custom_call_target="tpu_custom_call" | custom-call | tf_op jit(solution)/shard_map/hyena/pallas_call | solution.py:392
  52.6 0.7 %write_out.1 = (bf16[64,256]{1,0:T(8,128)(2,1)}, f32[1,256]{1,0:T(1,128)}, bf16[3,64,256]{2,1,0:T(8,128)(2,1)}, f32[64,256]{1,0:T(8,128)}) custom-call(bf16[64,256]{1,0:T(8,128)(2,1)S(1)} %get-tuple-element.12.refs_0_, f32[1,256]{1,0:T(1,128)S(1)} %get-tuple-element.13.refs_1_, bf16[3,64,256]{2,1,0:T(8,128)(2,1)S(1)} %get-tuple-element.14.refs_2_, ...), custom_call_target="tpu_custom_call" | custom-call | tf_op jit(solution)/shard_map/write_out/pallas_call | solution.py:443

commit v4 on v3

--- a/solution.py
+++ b/solution.py
@@ -29,17 +29,28 @@
     return sorted(((a, b) for a in range(4) for b in range(4) if a or b), key=lambda offset: -hops(offset))
 
 
-def fine_shifts(row, dst):
+def fine_shifts(row, dst, backward=False):
     width = row.shape[1]
     strip = pltpu.roll(jnp.broadcast_to(row, (8, width)), 0, 1, stride=1, stride_axis=0)
     lane = lax.broadcasted_iota(jnp.int32, (16, LANES), 1)
     sub = lax.broadcasted_iota(jnp.int32, (16, LANES), 0)
+    if backward:
+        strip = jnp.dot(exchange_matrix(8), strip.astype(jnp.bfloat16), preferred_element_type=jnp.float32)
     for k in range(LANES // 16):
-        low = strip if k == 0 else pltpu.roll(strip, 16 * k, 1)
-        both = jnp.concatenate([low, pltpu.roll(strip, 16 * k + 8, 1)], axis=0)
-        first = jnp.where(lane >= sub + 16 * k, both[:, :LANES], 0.0)
-        dst[16 * k : 16 * k + 16, :LANES] = first.astype(jnp.bfloat16)
+        if backward:
+            first, second, shift = LANES - 8 - 16 * k, LANES - 16 - 16 * k, LANES - 1 - 16 * k - sub
+        else:
+            first, second, shift = 16 * k, 16 * k + 8, 16 * k + sub
+        halves = [strip if by == 0 else pltpu.roll(strip, by, 1) for by in (first, second)]
+        both = jnp.concatenate(halves, axis=0)
+        start = jnp.where(lane >= shift, both[:, :LANES], 0.0)
+        dst[16 * k : 16 * k + 16, :LANES] = start.astype(jnp.bfloat16)
         dst[16 * k : 16 * k + 16, LANES:] = both[:, LANES:].astype(jnp.bfloat16)
+
+
+def exchange_matrix(size):
+    total = lax.broadcasted_iota(jnp.int32, (size, size), 0) + lax.broadcasted_iota(jnp.int32, (size, size), 1)
+    return (total == size - 1).astype(jnp.float32).astype(jnp.bfloat16)
 
 
 def kernel(
@@ -48,8 +59,8 @@
     so_ref, tm_ref, gr_ref, fg_ref,
     send_m, send_p, send_y, send_g, send_f,
     recv_m, recv_p, recv_y, recv_g, recv_f,
-    proj, scale, cot, reach_row, skip_row, wide_rows, aux, response,
-    taps_bf, taps, fine, pads, left, rev, turned,
+    proj, scale, cot, reach_row, skip_row, wide_rows, aux, response, factor, offset_term,
+    taps_bf, taps, fine, pads, left, ahead, turned,
     lm, win, wide, other,
     in_sem, ctx_send, ctx_recv, z_send, z_recv, core_sem, relay_sem,
 ):
@@ -136,8 +147,18 @@
     def pulled_of(half):
         return (upstream(half) * dequant(0, half)).astype(jnp.bfloat16).astype(jnp.float32)
 
-    for half in range(2):
-        send_m[pl.ds(half, chans, stride=2), :] = mixed_of(half)
+    flip = exchange_matrix(LANES)
+
+    def reverse(values):
+        return jnp.dot(values, flip, preferred_element_type=jnp.float32)
+
+    def reverse_wide(values):
+        top = values.astype(jnp.bfloat16)
+        rest = (values - top.astype(jnp.float32)).astype(jnp.bfloat16)
+        return reverse(top) + reverse(rest)
+
+    for half in range(2):
+        send_m[pl.ds(half, chans, stride=2), :] = reverse(mixed_of(half).astype(jnp.bfloat16))
         send_p[pl.ds(half, chans, stride=2), :] = pulled_of(half)
 
     mine = pl.ds(pl.multiple_of(rows * me, rows), rows)
@@ -153,8 +174,7 @@
                 device_id_type=MESH,
             )
 
-        def arrival(step):
-            peer = peer_of(step)
+        def arrival(peer):
             return pltpu.make_async_remote_copy(
                 src_ref=src.at[mine, :],
                 dst_ref=dst.at[pl.ds(pl.multiple_of(rows * peer, rows), rows), :],
@@ -178,10 +198,14 @@
 
         def wait_recv():
             def go(step, carry):
-                arrival(step).wait_recv()
+                arrival(peer_of(step)).wait_recv()
                 return carry
 
-            lax.fori_loop(1, parts, go, 0)
+            if urgent:
+                for peer in reversed(far_first):
+                    arrival(peer).wait_recv()
+            else:
+                lax.fori_loop(1, parts, go, 0)
 
         def wait_send():
             def go(step, carry):
@@ -202,7 +226,6 @@
     m_start()
     if relays:
         relay_send(0)
-    p_start()
 
     fetches[-1].wait()
     taps[...] = taps_bf[...].astype(jnp.float32)
@@ -210,28 +233,20 @@
     for j in range(own):
         row = taps[pl.ds(me % per_tile * own + j, 1), :]
         reach = aux[pl.ds(me * own + j, 1), :][:, 7:8]
-        fine_shifts(jnp.where(lag < reach, row, 0.0), fine.at[j, 0:LANES])
-
-    flip = (
-        lax.broadcasted_iota(jnp.int32, (LANES, LANES), 0)
-        + lax.broadcasted_iota(jnp.int32, (LANES, LANES), 1)
-        == LANES - 1
-    ).astype(jnp.float32).astype(jnp.bfloat16)
-
-    def reverse(values):
-        return jnp.dot(values, flip, preferred_element_type=jnp.float32)
-
-    m_recv()
+        fine_shifts(jnp.where(lag < reach, row, 0.0), fine.at[j, 0:LANES], backward=True)
+
+    p_start()
     if relays:
         relay_wait(0)
         relay_send(1)
-    rev[...] = reverse(recv_m[...].astype(jnp.bfloat16))
+
+    m_recv()
     zeros = jnp.zeros((parts, LANES), jnp.float32)
     for slot in range(2):
         pads[slot, 0:parts, :] = zeros
     for j in range(own):
-        pads[0, parts : 2 * parts, :] = rev[pl.ds(2 * j + 1, parts, stride=rows), :]
-        pads[1, parts : 2 * parts, :] = rev[pl.ds(2 * j, parts, stride=rows), :]
+        pads[0, parts : 2 * parts, :] = recv_m[pl.ds(2 * j + 1, parts, stride=rows), :]
+        pads[1, parts : 2 * parts, :] = recv_m[pl.ds(2 * j, parts, stride=rows), :]
         for n in range(2 * parts + 1):
             at = parts - n // 2
             block = pads[n % 2, at : at + parts, :].astype(jnp.bfloat16)
@@ -241,16 +256,12 @@
                 left[j, parts : 2 * parts, LANES * (n - 1) : LANES * n] = block
     for j in range(own):
         out = lax.dot_general(left[j], fine[j, 0:LANES, :], NT, preferred_element_type=jnp.float32)
-        turned[pl.ds(2 * j, parts, stride=rows), :] = out[parts:]
-        turned[pl.ds(2 * j + 1, parts, stride=rows), :] = out[:parts]
-    whole = turned[...]
-    top = whole.astype(jnp.bfloat16)
-    rest = (whole - top.astype(jnp.float32)).astype(jnp.bfloat16)
-    send_y[...] = reverse(top) + reverse(rest)
+        send_y[pl.ds(2 * j, parts, stride=rows), :] = out[parts:]
+        send_y[pl.ds(2 * j + 1, parts, stride=rows), :] = out[:parts]
     y_start()
 
     def gradients_of(j):
-        blocks = [recv_m[rows * c + 2 * j + half : rows * c + 2 * j + half + 1, :] for c in range(parts) for half in range(2)]
+        blocks = [ahead[rows * c + 2 * j + half : rows * c + 2 * j + half + 1, :] for c in range(parts) for half in range(2)]
         fine_shifts(jnp.concatenate(blocks, axis=1), fine.at[j, LANES : 2 * LANES])
         for half in range(2):
             pads[half, 0:parts, :] = recv_p[pl.ds(2 * j + half, parts, stride=rows), :]
@@ -265,23 +276,28 @@
         out = lax.dot_general(left[j], fine[j], NT, preferred_element_type=jnp.float32)
         for half in range(2):
             part = out[parts * half : parts * (half + 1)]
-            send_g[pl.ds(2 * j + half, parts, stride=rows), :] = part[:, :LANES]
+            turned[pl.ds(2 * j + half, parts, stride=rows), :] = part[:, :LANES]
             send_f[pl.ds(2 * j + half, parts, stride=rows), :] = part[:, LANES:]
 
+    ahead[...] = reverse(recv_m[...].astype(jnp.bfloat16))
+    gain = column(6)
+    for half in range(2):
+        query = dequant(0, half)
+        factor[:, LANES * half : LANES * (half + 1)] = query * fscale
+        offset_term[:, LANES * half : LANES * (half + 1)] = query * (gain * mixed_of(half))
     p_recv()
-    for j in range(own):
+    for j in range(own // 2):
         gradients_of(j)
 
     y_recv()
-    gain = column(6)
+    for half in range(2):
+        block = slice(LANES * half, LANES * (half + 1))
+        value = factor[:, block] * recv_y[pl.ds(half, chans, stride=2), :] + offset_term[:, block]
+        response[:, block] = value
+        lm[0, :, block] = jnp.max(jnp.abs(value), axis=0, keepdims=True)
 
     def conv_of(half):
         return recv_y[pl.ds(half, chans, stride=2), :] * fscale + gain * mixed_of(half)
-
-    for half in range(2):
-        value = dequant(0, half) * conv_of(half)
-        response[:, LANES * half : LANES * (half + 1)] = value
-        lm[0, :, LANES * half : LANES * (half + 1)] = jnp.max(jnp.abs(value), axis=0, keepdims=True)
 
     def z_step(index):
         return chips // 2 + (index + 1) // 2 * (1 - 2 * (index % 2))
@@ -323,6 +339,9 @@
         relay_wait(1)
     lax.fori_loop(0, chips - 1, z_start, 0)
     win[zpos] = lm[0]
+    for j in range(own // 2, own):
+        gradients_of(j)
+    send_g[...] = reverse_wide(turned[...])
     g_start()
     f_start()
 
@@ -403,6 +422,8 @@
             pltpu.VMEM((1, chans), jnp.float32),
             pltpu.VMEM((8, LANES), jnp.float32),
             pltpu.VMEM((chans, 8), jnp.float32),
+            pltpu.VMEM((chans, span), jnp.float32),
+            pltpu.VMEM((chans, span), jnp.float32),
             pltpu.VMEM((chans, span), jnp.float32),
             pltpu.VMEM((16, seq), jnp.bfloat16),
             pltpu.VMEM((16, seq), jnp.float32),

time: 53.4 us -> 52.9 us (level)
  no operation moved by 1% of the time
where the time goes in v4:
time: 52.9 us; the launch traced here: 52.8 us
  Pallas kernels  52.1 us (98%)
  between operations  0.64 us (1%)
    pallas_call x1, Pallas kernels, body(): pl.pallas_call(functools.partial(kernel, parts, chips, chans, seq), out_s...  51.4 us

profile of v4, /device:TPU:1, one launch (start us, length us, event | category | flops | bytes accessed | tf_op | source)
XLA Modules:
  0.0 52.8 jit_solution(9286677505608808340)
XLA Ops:
  0.6 51.4 %hyena.1 = (bf16[64,256]{1,0:T(8,128)(2,1)S(1)}, f32[1,256]{1,0:T(1,128)S(1)}, bf16[3,64,256]{2,1,0:T(8,128)(2,1)S(1)}, f32[64,256]{1,0:T(8,128)S(1)}) custom-call(bf16[3,64,256]{2,1,0:T(8,128)(2,1)} %proj_hbm.1, s32[3,2,64]{2,1,0:T(2,128)} %bitcast.4, bf16[64,256]{1,0:T(8,128)(2,1)} %cot_hbm.1, bf16[64,4096]{1,0:T(8,128)(2,1)} %filt.1, s32[1,64]{1,0:T(1,128)} %bitcast.5, ...), custom_call_target="tpu_custom_call" | custom-call | tf_op jit(solution)/shard_map/hyena/pallas_call | solution.py:411
  52.0 0.7 %write_out.1 = (bf16[64,256]{1,0:T(8,128)(2,1)}, f32[1,256]{1,0:T(1,128)}, bf16[3,64,256]{2,1,0:T(8,128)(2,1)}, f32[64,256]{1,0:T(8,128)}) custom-call(bf16[64,256]{1,0:T(8,128)(2,1)S(1)} %get-tuple-element.12.refs_0_, f32[1,256]{1,0:T(1,128)S(1)} %get-tuple-element.13.refs_1_, bf16[3,64,256]{2,1,0:T(8,128)(2,1)S(1)} %get-tuple-element.14.refs_2_, ...), custom_call_target="tpu_custom_call" | custom-call | tf_op jit(solution)/shard_map/write_out/pallas_call | solution.py:464

commit v5 on v4

--- a/solution.py
+++ b/solution.py
@@ -12,7 +12,6 @@
 MESH = pl.DeviceIdType.MESH
 LANES = 128
 CORES = 2
-NT = (((1,), (1,)), ((), ()))
 
 
 def z_greetings(chips):
@@ -21,31 +20,27 @@
     return tuple(range(chips)), ()
 
 
+def ctx_hops(offset):
+    return sum(min(part, 4 - part) for part in offset)
+
+
 def ctx_offsets(parts):
     if parts != 16:
         return None
-    def hops(offset):
-        return sum(min(part, 4 - part) for part in offset)
-    return sorted(((a, b) for a in range(4) for b in range(4) if a or b), key=lambda offset: -hops(offset))
-
-
-def fine_shifts(row, dst, backward=False):
+    return sorted(((a, b) for a in range(4) for b in range(4) if a or b), key=lambda offset: -ctx_hops(offset))
+
+
+def fine_shifts(row, dst):
     width = row.shape[1]
-    strip = pltpu.roll(jnp.broadcast_to(row, (8, width)), 0, 1, stride=1, stride_axis=0)
-    lane = lax.broadcasted_iota(jnp.int32, (16, LANES), 1)
-    sub = lax.broadcasted_iota(jnp.int32, (16, LANES), 0)
-    if backward:
-        strip = jnp.dot(exchange_matrix(8), strip.astype(jnp.bfloat16), preferred_element_type=jnp.float32)
+    total = width + LANES
+    padded = jnp.concatenate([jnp.zeros((1, LANES), jnp.float32), row], axis=1)
+    strip = pltpu.roll(jnp.broadcast_to(padded, (8, total)), 0, 1, stride=1, stride_axis=0)
+    strip = jnp.dot(exchange_matrix(8), strip.astype(jnp.bfloat16), preferred_element_type=jnp.float32)
     for k in range(LANES // 16):
-        if backward:
-            first, second, shift = LANES - 8 - 16 * k, LANES - 16 - 16 * k, LANES - 1 - 16 * k - sub
-        else:
-            first, second, shift = 16 * k, 16 * k + 8, 16 * k + sub
-        halves = [strip if by == 0 else pltpu.roll(strip, by, 1) for by in (first, second)]
-        both = jnp.concatenate(halves, axis=0)
-        start = jnp.where(lane >= shift, both[:, :LANES], 0.0)
-        dst[16 * k : 16 * k + 16, :LANES] = start.astype(jnp.bfloat16)
-        dst[16 * k : 16 * k + 16, LANES:] = both[:, LANES:].astype(jnp.bfloat16)
+        halves = [pltpu.roll(strip, total - by, 1) for by in (16 * k + 8, 16 * k + 16)]
+        both = jnp.concatenate(halves, axis=0).astype(jnp.bfloat16)
+        for n in range(width // LANES):
+            dst[LANES * n + 16 * k : LANES * n + 16 * k + 16, :] = both[:, LANES * n : LANES * (n + 1)]
 
 
 def exchange_matrix(size):
@@ -60,7 +55,7 @@
     send_m, send_p, send_y, send_g, send_f,
     recv_m, recv_p, recv_y, recv_g, recv_f,
     proj, scale, cot, reach_row, skip_row, wide_rows, aux, response, factor, offset_term,
-    taps_bf, taps, fine, pads, left, ahead, turned,
+    taps_bf, taps, fine, pads, left, ahead, turned_g, turned_f,
     lm, win, wide, other,
     in_sem, ctx_send, ctx_recv, z_send, z_recv, core_sem, relay_sem,
 ):
@@ -84,15 +79,17 @@
     offsets = ctx_offsets(parts)
     if offsets is None:
         far_first = [peer_of(step) for step in range(1, parts)]
+        targets = [(0, {"ctx": peer}) for peer in far_first]
     else:
         far_first = [lax.rem(me // 4 + a, 4) * 4 + lax.rem(me % 4 + b, 4) for a, b in offsets]
-    for peer in far_first:
-        pl.semaphore_signal(barrier, inc=1, device_id={"ctx": peer}, device_id_type=MESH)
-    greeted = parts - 1
+        targets = [(ctx_hops(offset), {"ctx": peer}) for offset, peer in zip(offsets, far_first)]
     for offset in near:
         for side in (1 - core,) if offset == 0 else tuple(range(CORES)):
-            pl.semaphore_signal(barrier, inc=1, device_id=chip_dev(offset, side), device_id_type=MESH)
-            greeted += 1
+            targets.append((abs(offset), chip_dev(offset, side)))
+    targets.sort(key=lambda target: -target[0])
+    for _, target in targets:
+        pl.semaphore_signal(barrier, inc=1, device_id=target, device_id_type=MESH)
+    greeted = len(targets)
 
     def relay_send(index):
         for offset in (-relays[index], relays[index]):
@@ -233,7 +230,7 @@
     for j in range(own):
         row = taps[pl.ds(me % per_tile * own + j, 1), :]
         reach = aux[pl.ds(me * own + j, 1), :][:, 7:8]
-        fine_shifts(jnp.where(lag < reach, row, 0.0), fine.at[j, 0:LANES], backward=True)
+        fine_shifts(jnp.where(lag < reach, row, 0.0), fine.at[j, :, 0:LANES])
 
     p_start()
     if relays:
@@ -255,14 +252,14 @@
             if n >= 1:
                 left[j, parts : 2 * parts, LANES * (n - 1) : LANES * n] = block
     for j in range(own):
-        out = lax.dot_general(left[j], fine[j, 0:LANES, :], NT, preferred_element_type=jnp.float32)
+        out = jnp.dot(left[j], fine[j, :, 0:LANES], preferred_element_type=jnp.float32)
         send_y[pl.ds(2 * j, parts, stride=rows), :] = out[parts:]
         send_y[pl.ds(2 * j + 1, parts, stride=rows), :] = out[:parts]
     y_start()
 
     def gradients_of(j):
         blocks = [ahead[rows * c + 2 * j + half : rows * c + 2 * j + half + 1, :] for c in range(parts) for half in range(2)]
-        fine_shifts(jnp.concatenate(blocks, axis=1), fine.at[j, LANES : 2 * LANES])
+        fine_shifts(jnp.concatenate(blocks, axis=1), fine.at[j, :, LANES : 2 * LANES])
         for half in range(2):
             pads[half, 0:parts, :] = recv_p[pl.ds(2 * j + half, parts, stride=rows), :]
             pads[half, parts : 2 * parts, :] = zeros
@@ -273,11 +270,11 @@
                 left[j, 0:parts, LANES * n : LANES * (n + 1)] = block
             if n >= 1:
                 left[j, parts : 2 * parts, LANES * (n - 1) : LANES * n] = block
-        out = lax.dot_general(left[j], fine[j], NT, preferred_element_type=jnp.float32)
+        out = jnp.dot(left[j], fine[j], preferred_element_type=jnp.float32)
         for half in range(2):
             part = out[parts * half : parts * (half + 1)]
-            turned[pl.ds(2 * j + half, parts, stride=rows), :] = part[:, :LANES]
-            send_f[pl.ds(2 * j + half, parts, stride=rows), :] = part[:, LANES:]
+            turned_g[pl.ds(2 * j + half, parts, stride=rows), :] = part[:, :LANES]
+            turned_f[pl.ds(2 * j + half, parts, stride=rows), :] = part[:, LANES:]
 
     ahead[...] = reverse(recv_m[...].astype(jnp.bfloat16))
     gain = column(6)
@@ -341,8 +338,9 @@
     win[zpos] = lm[0]
     for j in range(own // 2, own):
         gradients_of(j)
-    send_g[...] = reverse_wide(turned[...])
+    send_g[...] = reverse_wide(turned_g[...])
     g_start()
+    send_f[...] = reverse_wide(turned_f[...])
     f_start()
 
     for half in range(2):
@@ -427,9 +425,10 @@
             pltpu.VMEM((chans, span), jnp.float32),
             pltpu.VMEM((16, seq), jnp.bfloat16),
             pltpu.VMEM((16, seq), jnp.float32),
-            pltpu.VMEM((own, 2 * LANES, seq), jnp.bfloat16),
+            pltpu.VMEM((own, seq, 2 * LANES), jnp.bfloat16),
             pltpu.VMEM((2, 2 * parts, LANES), jnp.float32),
             pltpu.VMEM((own, 2 * parts, seq), jnp.bfloat16),
+            slab,
             slab,
             slab,
             pltpu.VMEM((1, 1, span), jnp.float32),

time: 52.9 us -> 52.3 us (0.989)
  Pallas kernels: 52.1 us -> 51.5 us
    pallas_call x1, Pallas kernels: 51.4 us -> 50.8 us  [body(): pl.pallas_call(functools.partial(kernel, parts, chips, chans, seq), out_s...]
where the time goes in v5:
time: 52.3 us; the launch traced here: 52.2 us
  Pallas kernels  51.5 us (98%)
  between operations  0.64 us (1%)
    pallas_call x1, Pallas kernels, body(): pl.pallas_call(functools.partial(kernel, parts, chips, chans, seq), out_s...  50.8 us

profile of v5, /device:TPU:1, one launch (start us, length us, event | category | flops | bytes accessed | tf_op | source)
XLA Modules:
  0.0 52.2 jit_solution(9565595213850045336)
XLA Ops:
  0.6 50.8 %hyena.1 = (bf16[64,256]{1,0:T(8,128)(2,1)S(1)}, f32[1,256]{1,0:T(1,128)S(1)}, bf16[3,64,256]{2,1,0:T(8,128)(2,1)S(1)}, f32[64,256]{1,0:T(8,128)S(1)}) custom-call(bf16[3,64,256]{2,1,0:T(8,128)(2,1)} %proj_hbm.1, s32[3,2,64]{2,1,0:T(2,128)} %bitcast.4, bf16[64,256]{1,0:T(8,128)(2,1)} %cot_hbm.1, bf16[64,4096]{1,0:T(8,128)(2,1)} %filt.1, s32[1,64]{1,0:T(1,128)} %bitcast.5, ...), custom_call_target="tpu_custom_call" | custom-call | tf_op jit(solution)/shard_map/hyena/pallas_call | solution.py:409
  51.4 0.7 %write_out.1 = (bf16[64,256]{1,0:T(8,128)(2,1)}, f32[1,256]{1,0:T(1,128)}, bf16[3,64,256]{2,1,0:T(8,128)(2,1)}, f32[64,256]{1,0:T(8,128)}) custom-call(bf16[64,256]{1,0:T(8,128)(2,1)S(1)} %get-tuple-element.12.refs_0_, f32[1,256]{1,0:T(1,128)S(1)} %get-tuple-element.13.refs_1_, bf16[3,64,256]{2,1,0:T(8,128)(2,1)S(1)} %get-tuple-element.14.refs_2_, ...), custom_call_target="tpu_custom_call" | custom-call | tf_op jit(solution)/shard_map/write_out/pallas_call | solution.py:463

commit v6 on v5

--- a/solution.py
+++ b/solution.py
@@ -56,8 +56,8 @@
     recv_m, recv_p, recv_y, recv_g, recv_f,
     proj, scale, cot, reach_row, skip_row, wide_rows, aux, response, factor, offset_term,
     taps_bf, taps, fine, pads, left, ahead, turned_g, turned_f,
-    lm, win, wide, other,
-    in_sem, ctx_send, ctx_recv, z_send, z_recv, core_sem, relay_sem,
+    lm, win,
+    in_sem, ctx_send, ctx_recv, z_send, z_recv, relay_sem,
 ):
     own = chans // parts
     rows = 2 * own
@@ -220,9 +220,9 @@
     f_start, f_recv, f_sent = exchange(4, send_f, recv_f)
 
     pl.semaphore_wait(barrier, greeted)
-    m_start()
     if relays:
         relay_send(0)
+    m_start()
 
     fetches[-1].wait()
     taps[...] = taps_bf[...].astype(jnp.float32)
@@ -282,16 +282,15 @@
         query = dequant(0, half)
         factor[:, LANES * half : LANES * (half + 1)] = query * fscale
         offset_term[:, LANES * half : LANES * (half + 1)] = query * (gain * mixed_of(half))
-    p_recv()
-    for j in range(own // 2):
-        gradients_of(j)
 
     y_recv()
+    peaks = []
     for half in range(2):
         block = slice(LANES * half, LANES * (half + 1))
         value = factor[:, block] * recv_y[pl.ds(half, chans, stride=2), :] + offset_term[:, block]
         response[:, block] = value
-        lm[0, :, block] = jnp.max(jnp.abs(value), axis=0, keepdims=True)
+        peaks.append(jnp.max(jnp.abs(value), axis=0, keepdims=True))
+    lm[0] = jnp.concatenate(peaks, axis=0).astype(jnp.bfloat16)
 
     def conv_of(half):
         return recv_y[pl.ds(half, chans, stride=2), :] * fscale + gain * mixed_of(half)
@@ -299,44 +298,49 @@
     def z_step(index):
         return chips // 2 + (index + 1) // 2 * (1 - 2 * (index % 2))
 
-    def z_push(step):
+    def z_push(step, side):
         return pltpu.make_async_remote_copy(
             src_ref=lm.at[0],
-            dst_ref=win.at[zpos],
-            send_sem=z_send.at[step],
-            recv_sem=z_recv.at[zpos],
-            device_id=chip_dev(step, core),
+            dst_ref=win.at[ch],
+            send_sem=z_send.at[CORES * step + side],
+            recv_sem=z_recv.at[ch],
+            device_id=chip_dev(step, side),
             device_id_type=MESH,
         )
 
-    def z_land(step):
-        origin = lax.rem(zpos + step, chips)
+    def z_land(step, side):
+        origin = lax.rem(zpos + step, chips) * CORES + side
         return pltpu.make_async_remote_copy(
             src_ref=lm.at[0],
             dst_ref=win.at[origin],
-            send_sem=z_send.at[step],
+            send_sem=z_send.at[CORES * step + side],
             recv_sem=z_recv.at[origin],
-            device_id=chip_dev(step, core),
+            device_id=chip_dev(step, side),
             device_id_type=MESH,
         )
 
     def z_start(index, carry):
-        z_push(z_step(index)).start()
+        for side in range(CORES):
+            z_push(z_step(index), side).start()
         return carry
 
     def z_arrive(index, carry):
-        z_land(z_step(chips - 2 - index)).wait_recv()
+        for side in range(CORES):
+            z_land(z_step(chips - 2 - index), side).wait_recv()
         return carry
 
     def z_sent(index, carry):
-        z_push(z_step(index)).wait_send()
+        for side in range(CORES):
+            z_push(z_step(index), side).wait_send()
         return carry
 
     if relays:
         relay_wait(1)
     lax.fori_loop(0, chips - 1, z_start, 0)
-    win[zpos] = lm[0]
-    for j in range(own // 2, own):
+    z_push(0, 1 - core).start()
+    win[ch] = lm[0]
+    p_recv()
+    for j in range(own):
         gradients_of(j)
     send_g[...] = reverse_wide(turned_g[...])
     g_start()
@@ -359,26 +363,17 @@
         )
 
 
+    z_land(0, 1 - core).wait_recv()
     lax.fori_loop(0, chips - 1, z_arrive, 0)
-    wide[0] = jnp.max(win[...], axis=0)
-    swap = pltpu.make_async_remote_copy(
-        src_ref=wide.at[0],
-        dst_ref=other.at[0],
-        send_sem=core_sem.at[0],
-        recv_sem=core_sem.at[1],
-        device_id=chip_dev(0, 1 - core),
-        device_id_type=MESH,
-    )
-    swap.start()
-    swap.wait_recv()
-    largest = jnp.maximum(wide[0], other[0])
+    pair = jnp.max(win[...].astype(jnp.float32), axis=0)
+    largest = jnp.concatenate([pair[0:1], pair[1:2]], axis=1)
     tm_ref[...] = largest
     so_ref[...] = (response[...] / (largest + 1e-06)).astype(so_ref.dtype)
 
     for sent in (m_sent, p_sent, y_sent, g_sent, f_sent):
         sent()
     lax.fori_loop(0, chips - 1, z_sent, 0)
-    swap.wait_send()
+    z_push(0, 1 - core).wait_send()
 
 
 def write_out(*refs):
@@ -431,16 +426,13 @@
             slab,
             slab,
             slab,
-            pltpu.VMEM((1, 1, span), jnp.float32),
-            pltpu.VMEM((chips, 1, span), jnp.float32),
-            pltpu.VMEM((1, 1, span), jnp.float32),
-            pltpu.VMEM((1, 1, span), jnp.float32),
+            pltpu.VMEM((1, 2, LANES), jnp.bfloat16),
+            pltpu.VMEM((CORES * chips, 2, LANES), jnp.bfloat16),
             pltpu.SemaphoreType.DMA((6,)),
             pltpu.SemaphoreType.DMA((5, parts)),
             pltpu.SemaphoreType.DMA((5, parts)),
-            pltpu.SemaphoreType.DMA((chips,)),
-            pltpu.SemaphoreType.DMA((chips,)),
-            pltpu.SemaphoreType.DMA((2,)),
+            pltpu.SemaphoreType.DMA((CORES * chips,)),
+            pltpu.SemaphoreType.DMA((CORES * chips,)),
             pltpu.SemaphoreType.REGULAR((2,)),
         ],
         compiler_params=pltpu.CompilerParams(

time: 52.3 us -> 51.6 us (0.987)
  Pallas kernels: 51.5 us -> 50.8 us
    pallas_call x1, Pallas kernels: 50.8 us -> 50.1 us  [body(): pl.pallas_call(functools.partial(kernel, parts, chips, chans, seq), out_s...]
where the time goes in v6:
time: 51.6 us; the launch traced here: 51.4 us
  Pallas kernels  50.8 us (98%)
  between operations  0.64 us (1%)
    pallas_call x1, Pallas kernels, body(): pl.pallas_call(functools.partial(kernel, parts, chips, chans, seq), out_s...  50.1 us

profile of v6, /device:TPU:1, one launch (start us, length us, event | category | flops | bytes accessed | tf_op | source)
XLA Modules:
  0.0 51.4 jit_solution(10521149186135031372)
XLA Ops:
  0.6 50.1 %hyena.1 = (bf16[64,256]{1,0:T(8,128)(2,1)S(1)}, f32[1,256]{1,0:T(1,128)S(1)}, bf16[3,64,256]{2,1,0:T(8,128)(2,1)S(1)}, f32[64,256]{1,0:T(8,128)S(1)}) custom-call(bf16[3,64,256]{2,1,0:T(8,128)(2,1)} %proj_hbm.1, s32[3,2,64]{2,1,0:T(2,128)} %bitcast.4, bf16[64,256]{1,0:T(8,128)(2,1)} %cot_hbm.1, bf16[64,4096]{1,0:T(8,128)(2,1)} %filt.1, s32[1,64]{1,0:T(1,128)} %bitcast.5, ...), custom_call_target="tpu_custom_call" | custom-call | tf_op jit(solution)/shard_map/hyena/pallas_call | solution.py:404
  50.7 0.7 %write_out.1 = (bf16[64,256]{1,0:T(8,128)(2,1)}, f32[1,256]{1,0:T(1,128)}, bf16[3,64,256]{2,1,0:T(8,128)(2,1)}, f32[64,256]{1,0:T(8,128)}) custom-call(bf16[64,256]{1,0:T(8,128)(2,1)S(1)} %get-tuple-element.12.refs_0_, f32[1,256]{1,0:T(1,128)S(1)} %get-tuple-element.13.refs_1_, bf16[3,64,256]{2,1,0:T(8,128)(2,1)S(1)} %get-tuple-element.14.refs_2_, ...), custom_call_target="tpu_custom_call" | custom-call | tf_op jit(solution)/shard_map/write_out/pallas_call | solution.py:455

commit v7 on v6

--- a/solution.py
+++ b/solution.py
@@ -363,17 +363,17 @@
         )
 
 
+    for sent in (m_sent, p_sent, y_sent, g_sent, f_sent):
+        sent()
+    lax.fori_loop(0, chips - 1, z_sent, 0)
+    z_push(0, 1 - core).wait_send()
+
     z_land(0, 1 - core).wait_recv()
     lax.fori_loop(0, chips - 1, z_arrive, 0)
     pair = jnp.max(win[...].astype(jnp.float32), axis=0)
     largest = jnp.concatenate([pair[0:1], pair[1:2]], axis=1)
     tm_ref[...] = largest
     so_ref[...] = (response[...] / (largest + 1e-06)).astype(so_ref.dtype)
-
-    for sent in (m_sent, p_sent, y_sent, g_sent, f_sent):
-        sent()
-    lax.fori_loop(0, chips - 1, z_sent, 0)
-    z_push(0, 1 - core).wait_send()
 
 
 def write_out(*refs):

time: 51.6 us -> 50.1 us (0.971)
  Pallas kernels: 50.8 us -> 49.2 us
    pallas_call x1, Pallas kernels: 50.1 us -> 48.5 us  [body(): pl.pallas_call(functools.partial(kernel, parts, chips, chans, seq), out_s...]
where the time goes in v7:
time: 50.1 us; the launch traced here: 49.9 us
  Pallas kernels  49.2 us (98%)
  between operations  0.64 us (1%)
    pallas_call x1, Pallas kernels, body(): pl.pallas_call(functools.partial(kernel, parts, chips, chans, seq), out_s...  48.5 us

profile of v7, /device:TPU:1, one launch (start us, length us, event | category | flops | bytes accessed | tf_op | source)
XLA Modules:
  0.0 49.9 jit_solution(15544540909753129749)
XLA Ops:
  0.6 48.5 %hyena.1 = (bf16[64,256]{1,0:T(8,128)(2,1)S(1)}, f32[1,256]{1,0:T(1,128)S(1)}, bf16[3,64,256]{2,1,0:T(8,128)(2,1)S(1)}, f32[64,256]{1,0:T(8,128)S(1)}) custom-call(bf16[3,64,256]{2,1,0:T(8,128)(2,1)} %proj_hbm.1, s32[3,2,64]{2,1,0:T(2,128)} %bitcast.4, bf16[64,256]{1,0:T(8,128)(2,1)} %cot_hbm.1, bf16[64,4096]{1,0:T(8,128)(2,1)} %filt.1, s32[1,64]{1,0:T(1,128)} %bitcast.5, ...), custom_call_target="tpu_custom_call" | custom-call | tf_op jit(solution)/shard_map/hyena/pallas_call | solution.py:404
  49.2 0.7 %write_out.1 = (bf16[64,256]{1,0:T(8,128)(2,1)}, f32[1,256]{1,0:T(1,128)}, bf16[3,64,256]{2,1,0:T(8,128)(2,1)}, f32[64,256]{1,0:T(8,128)}) custom-call(bf16[64,256]{1,0:T(8,128)(2,1)S(1)} %get-tuple-element.12.refs_0_, f32[1,256]{1,0:T(1,128)S(1)} %get-tuple-element.13.refs_1_, bf16[3,64,256]{2,1,0:T(8,128)(2,1)S(1)} %get-tuple-element.14.refs_2_, ...), custom_call_target="tpu_custom_call" | custom-call | tf_op jit(solution)/shard_map/write_out/pallas_call | solution.py:455
